TPU v7x, 32 devices: a whole 2x2x4 slice. The times are simulated.
32 devices in a mesh: gx: 4 (over y, x), gy: 8 (over z, core).
Axes of the slice: x: 2, y: 2, z: 4, core: 2. Of those that a mesh axis runs over, the one named last changes fastest.
Arguments:
- operator_t: bfloat16 [64, 512, 2432], P('gx', 'gy'), may hold values from -0.046875 to 0.046875
- data_columns: bfloat16 [2432, 384], P(('gx', 'gy')), may hold values from -6 to 6
- noise_var: float32 [2432], P(('gx', 'gy')), may hold values from 0.05 to 0.5
- class_map: int32 [64, 512], P('gx', 'gy'), may hold values from 0 to 15
- diffusion_table: float32 [16], replicated, may hold values from 0.5 to 4
- kappa_table: float32 [16], replicated, may hold values from 0.02 to 0.3
Outputs:
- hessian_block: float32 [2432, 384], P(('gx', 'gy'))
- prior_field: float32 [64, 512, 384], P('gx', 'gy')
All inputs are finite; a program needn't handle non-finite values.
Results may differ from a plain program's by a relative error of at most 0.0003.
Values may be sent and summed in bfloat16 or wider, within the bound.
A program may use at most 64 MiB of HBM per device.

v0:
```python
import jax
import jax.numpy as jnp
from jax import lax
from jax.sharding import PartitionSpec as P

ITERS = 8


def padded_2(block, sides, width):
    for axis, dim in sides:
        count = lax.axis_size(axis)
        forward = [(i, i + 1) for i in range(count - 1)]
        backward = [(target, source) for source, target in forward]
        low = lax.ppermute(
            lax.slice_in_dim(block, block.shape[dim] - width, None, axis=dim), axis, forward
        )
        high = lax.ppermute(lax.slice_in_dim(block, 0, width, axis=dim), axis, backward)
        block = jnp.concatenate([low, block, high], axis=dim)
    return block


def lookup(classes, entries):
    onehot = (classes[..., None] == jnp.arange(entries.shape[0], dtype=jnp.int32)).astype(
        jnp.float32
    )
    return jnp.sum(onehot * entries, axis=-1)


def edge_weights(padded):
    centre = padded[1:-1, 1:-1]
    north_w = 0.5 * (centre + padded[:-2, 1:-1])
    south_w = 0.5 * (centre + padded[2:, 1:-1])
    west_w = 0.5 * (centre + padded[1:-1, :-2])
    east_w = 0.5 * (centre + padded[1:-1, 2:])
    return (north_w, south_w, west_w, east_w)


def jacobi_step(source, padded, weights, divisor):
    summed = source + weights[0][..., None] * padded[:-2, 1:-1]
    summed = summed + weights[1][..., None] * padded[2:, 1:-1]
    summed = summed + weights[2][..., None] * padded[1:-1, :-2]
    summed = summed + weights[3][..., None] * padded[1:-1, 2:]
    return summed / divisor[..., None]


def local(operator_t, data_columns, noise_var, class_map, diffusion_table, kappa_table):
    tile_rows, tile_cols, data_rows = operator_t.shape
    columns_count = data_columns.shape[1]
    flattened = operator_t.reshape(tile_rows * tile_cols, data_rows)
    selected = flattened
    source = jnp.dot(
        selected,
        lax.all_gather(data_columns, ("gx", "gy"), axis=0, tiled=True),
        preferred_element_type=jnp.float32,
    )
    source = source.reshape(tile_rows, tile_cols, columns_count)
    diffusion = lookup(class_map, diffusion_table)
    reaction = lookup(class_map, kappa_table)
    margin = ITERS
    stacked = padded_2(jnp.stack([diffusion, reaction]), (("gx", 1), ("gy", 2)), margin + 1)
    weights = edge_weights(stacked[0])
    reaction_ext = stacked[1, 1:-1, 1:-1]
    extended = padded_2(source, (("gx", 0), ("gy", 1)), margin)
    global_rows = (
        lax.axis_index("gx") * tile_rows
        + jnp.arange(tile_rows + 2 * margin, dtype=jnp.int32)
        - margin
    )
    global_cols = (
        lax.axis_index("gy") * tile_cols
        + jnp.arange(tile_cols + 2 * margin, dtype=jnp.int32)
        - margin
    )
    rows_inside = (global_rows >= 0) & (global_rows < tile_rows * lax.axis_size("gx"))
    cols_inside = (global_cols >= 0) & (global_cols < tile_cols * lax.axis_size("gy"))
    inside = rows_inside[:, None] & cols_inside[None, :]
    divisor = jnp.where(
        inside, reaction_ext + weights[0] + weights[1] + weights[2] + weights[3], 1.0
    )
    retained = inside.astype(jnp.float32)[..., None]
    iterate = extended / divisor[..., None] * retained
    for repeat in range(ITERS):
        padded = jnp.pad(iterate, ((1, 1), (1, 1), (0, 0)))
        iterate = jacobi_step(extended, padded, weights, divisor) * retained
    iterate = iterate[margin : margin + tile_rows, margin : margin + tile_cols]
    smooth = iterate.astype(jnp.bfloat16).reshape(tile_rows * tile_cols, columns_count)
    selected = flattened
    forward = lax.psum_scatter(
        lax.dot_general(
            selected, smooth, (((0,), (0,)), ((), ())), preferred_element_type=jnp.float32
        ),
        ("gx", "gy"),
        scatter_dimension=0,
        tiled=True,
    )
    return (forward + noise_var[:, None] * data_columns.astype(jnp.float32), iterate)


def solution(mesh):
    placed = (P("gx", "gy", None), P(("gx", "gy"), None), P(("gx", "gy")), P("gx", "gy"), P(), P())
    return jax.shard_map(
        local,
        mesh=mesh,
        in_specs=placed,
        out_specs=(P(("gx", "gy"), None), P("gx", "gy", None)),
        check_vma=False,
    )
```

profile of v0, /device:TPU:0, one launch (start us, length us, event | category | flops | bytes accessed | tf_op | source)
XLA Modules:
  0.0 314.7 jit_solution(3147756326322825529)
XLA Ops:
  7.2 0.0 all-gather.3.cloned.1.call-start
  7.2 0.7 all-gather.3.cloned.1.call-update
  7.9 0.0 all-reduce.11.cloned.1.call-start
  7.9 0.8 select_reduce_fusion.1
  8.8 4.9 %collective-permute-start.4 = (f32[2,9,64]{2,1,0:T(8,128)S(1)}, f32[2,9,64]{2,1,0:T(8,128)S(1)}, u32[]{:S(2)}, u32[]{:S(2)}) collective-permute-start(f32[2,9,64]{2,1,0:T(8,128)S(1)} %get-tuple-element.29), channel_id=1, source_target_pairs={{0,8},{8,16},{16,24},{1,9},{9,17},{17,25},{2,10},{10,18},{18,26},{... | collective-permute-start | bytes 13832 | tf_op jit(solution)/shard_map/ppermute | solution.py:14
  13.7 1.3 collective-permute-start.5
  15.0 55.0 %all-gather.3.cloned.1.call-done = bf16[32,76,384]{2,1,0:T(8,128)(2,1)} async-done(((bf16[1,76,384]{2,1,0:T(8,128)(2,1)}), bf16[32,76,384]{2,1,0:T(8,128)(2,1)}) %all-gather.3.cloned.1.call-update) | async-done | bytes 1867792 | tf_op jit(solution)/shard_map/all_gather | solution.py:53
  70.0 2.5 reshape.69
  72.4 4.7 %fusion.91 = f32[1024,384]{1,0:T(8,128)S(1)} fusion(bf16[1024,2432]{1,0:T(8,128)(2,1)} %bitcast.39, bf16[2432,384]{1,0:T(8,128)(2,1)S(1)} %reshape.69), kind=kOutput, calls=%fused_computation.147 | convolution fusion | flops 1912602624 | bytes 8421376 | tf_op jit(solution)/shard_map/dot_general | solution.py:51
  77.1 0.1 fusion.89
  77.2 3.3 %collective-permute-start = (f32[8,64,384]{2,1,0:T(8,128)S(1)}, f32[8,64,384]{2,1,0:T(8,128)S(1)}, u32[]{:S(2)}, u32[]{:S(2)}) collective-permute-start(f32[8,64,384]{2,1,0:T(8,128)S(1)} %bitcast.43), channel_id=1, source_target_pairs={{0,8},{8,16},{16,24},{1,9},{9,17},{17,25},{2,10},{10,18},{18,26},{... | collective-permute-start | bytes 2359304 | tf_op jit(solution)/shard_map/ppermute | solution.py:14
  80.5 1.3 collective-permute-start.1
  81.9 0.1 fusion.90
  82.0 1.8 collective-permute-start.6
  83.8 1.3 collective-permute-start.7
  85.1 0.1 and_convert_fusion
  85.2 0.1 slice.221
  85.3 1.8 collective-permute-done.7
  87.1 0.1 pad_maximum_fusion.5
  87.2 10.5 %collective-permute-done = f32[8,64,384]{2,1,0:T(8,128)S(1)} collective-permute-done((f32[8,64,384]{2,1,0:T(8,128)S(1)}, f32[8,64,384]{2,1,0:T(8,128)S(1)}, u32[]{:S(2)}, u32[]{:S(2)}) %collective-permute-start) | collective-permute-done | bytes 786464 | tf_op jit(solution)/shard_map/ppermute | solution.py:14
  97.7 18.9 %collective-permute-done.1 = f32[8,64,384]{2,1,0:T(8,128)S(1)} collective-permute-done((f32[8,64,384]{2,1,0:T(8,128)S(1)}, f32[8,64,384]{2,1,0:T(8,128)S(1)}, u32[]{:S(2)}, u32[]{:S(2)}) %collective-permute-start.1) | collective-permute-done | bytes 786464 | tf_op jit(solution)/shard_map/ppermute | solution.py:17
  116.5 0.1 pad_maximum_fusion.3
  116.6 1.3 collective-permute-start.2
  117.9 1.3 collective-permute-start.3
  119.2 0.1 and_select_fusion
  119.4 0.1 slice.214
  119.4 0.1 slice.216
  119.5 0.1 slice.218
  119.6 0.1 slice.220
  119.7 2.6 collective-permute-done.3
  122.2 1.2 pad_maximum_fusion
  123.5 3.8 %fusion.70 = f32[32,80,384]{2,1,0:T(8,128)S(1)} fusion(f32[32,80,384]{2,1,0:T(8,128)S(1)} %get-tuple-element.18, f32[32,80]{1,0:T(8,128)S(1)} %get-tuple-element.16, f32[32,80]{1,0:T(8,128)S(1)} %get-tuple-element.15, f32[32,80]{1,0:T(8,128)S(1)} %get-tuple-element.14, f32[32,80]{1,0:T(8,128)S(1)} %and_convert_fusion, f32[32,80]{1,0:T(8,128)S(1)} %get-tuple-element.12, ...), kind=kLoop, calls=%fused_computation.105 | loop fusion | flops 13762560 | bytes 11857920 | tf_op jit(solution)/shard_map/mul | solution.py:84
  127.3 3.8 %fusion.69 = f32[32,80,384]{2,1,0:T(8,128)S(1)} fusion(f32[32,80,384]{2,1,0:T(8,128)S(1)} %fusion.70, f32[32,80]{1,0:T(8,128)S(1)} %get-tuple-element.16, f32[32,80]{1,0:T(8,128)S(1)} %get-tuple-element.15, f32[32,80]{1,0:T(8,128)S(1)} %get-tuple-element.14, f32[32,80]{1,0:T(8,128)S(1)} %and_convert_fusion, f32[32,80]{1,0:T(8,128)S(1)} %get-tuple-element.12, ...), kind=kLoop, calls=%fused_computation.104 | loop fusion | flops 13762560 | bytes 11857920 | tf_op jit(solution)/shard_map/mul | solution.py:84
  131.1 3.8 %fusion.68 = f32[32,80,384]{2,1,0:T(8,128)S(1)} fusion(f32[32,80,384]{2,1,0:T(8,128)S(1)} %fusion.69, f32[32,80]{1,0:T(8,128)S(1)} %get-tuple-element.16, f32[32,80]{1,0:T(8,128)S(1)} %get-tuple-element.15, f32[32,80]{1,0:T(8,128)S(1)} %get-tuple-element.14, f32[32,80]{1,0:T(8,128)S(1)} %and_convert_fusion, f32[32,80]{1,0:T(8,128)S(1)} %get-tuple-element.12, ...), kind=kLoop, calls=%fused_computation.103 | loop fusion | flops 13762560 | bytes 11857920 | tf_op jit(solution)/shard_map/mul | solution.py:84
  134.9 3.8 %fusion.67 = f32[32,80,384]{2,1,0:T(8,128)S(1)} fusion(f32[32,80,384]{2,1,0:T(8,128)S(1)} %fusion.68, f32[32,80]{1,0:T(8,128)S(1)} %get-tuple-element.16, f32[32,80]{1,0:T(8,128)S(1)} %get-tuple-element.15, f32[32,80]{1,0:T(8,128)S(1)} %get-tuple-element.14, f32[32,80]{1,0:T(8,128)S(1)} %and_convert_fusion, f32[32,80]{1,0:T(8,128)S(1)} %get-tuple-element.12, ...), kind=kLoop, calls=%fused_computation.102 | loop fusion | flops 13762560 | bytes 11857920 | tf_op jit(solution)/shard_map/mul | solution.py:84
  138.7 3.8 %fusion.66 = f32[32,80,384]{2,1,0:T(8,128)S(1)} fusion(f32[32,80,384]{2,1,0:T(8,128)S(1)} %fusion.67, f32[32,80]{1,0:T(8,128)S(1)} %get-tuple-element.16, f32[32,80]{1,0:T(8,128)S(1)} %get-tuple-element.15, f32[32,80]{1,0:T(8,128)S(1)} %get-tuple-element.14, f32[32,80]{1,0:T(8,128)S(1)} %and_convert_fusion, f32[32,80]{1,0:T(8,128)S(1)} %get-tuple-element.12, ...), kind=kLoop, calls=%fused_computation.101 | loop fusion | flops 13762560 | bytes 11857920 | tf_op jit(solution)/shard_map/mul | solution.py:84
  142.5 3.8 %fusion.65 = f32[32,80,384]{2,1,0:T(8,128)S(1)} fusion(f32[32,80,384]{2,1,0:T(8,128)S(1)} %fusion.66, f32[32,80]{1,0:T(8,128)S(1)} %get-tuple-element.16, f32[32,80]{1,0:T(8,128)S(1)} %get-tuple-element.15, f32[32,80]{1,0:T(8,128)S(1)} %get-tuple-element.14, f32[32,80]{1,0:T(8,128)S(1)} %and_convert_fusion, f32[32,80]{1,0:T(8,128)S(1)} %get-tuple-element.12, ...), kind=kLoop, calls=%fused_computation.100 | loop fusion | flops 13762560 | bytes 11857920 | tf_op jit(solution)/shard_map/mul | solution.py:84
  146.2 0.0 slice-start
  146.3 3.8 %fusion.64 = f32[32,80,384]{2,1,0:T(8,128)S(1)} fusion(f32[32,80,384]{2,1,0:T(8,128)S(1)} %fusion.65, f32[32,80]{1,0:T(8,128)S(1)} %get-tuple-element.16, f32[32,80]{1,0:T(8,128)S(1)} %get-tuple-element.15, f32[32,80]{1,0:T(8,128)S(1)} %get-tuple-element.14, f32[32,80]{1,0:T(8,128)S(1)} %and_convert_fusion, f32[32,80]{1,0:T(8,128)S(1)} %get-tuple-element.12, ...), kind=kLoop, calls=%fused_computation.99 | loop fusion | flops 13762560 | bytes 11857920 | tf_op jit(solution)/shard_map/mul | solution.py:84
  150.0 0.0 slice-start.1
  150.0 4.7 %fusion.63 = (f32[32,80,384]{2,1,0:T(8,128)S(1)}, f32[32,80,384]{2,1,0:T(8,128)}, f32[32,80,384]{2,1,0:T(8,128)}, f32[32,80,384]{2,1,0:T(8,128)}) fusion(f32[32,80,384]{2,1,0:T(8,128)S(1)} %fusion.64, f32[32,80]{1,0:T(8,128)S(1)} %get-tuple-element.13), kind=kLoop, calls=%fused_computation.96 | loop fusion | flops 983040 | bytes 19671040 | tf_op jit(solution)/shard_map/mul | solution.py:39
  154.8 2.8 fusion.73
  157.7 4.2 %convolution_bitcast_fusion = f32[2432,384]{0,1:T(8,128)} fusion(bf16[16,64,2432]{2,1,0:T(8,128)(2,1)S(1)} %bitcast.41, f32[16,64,384]{2,1,0:T(8,128)S(1)} %fusion.73), kind=kOutput, calls=%fused_computation.32 | convolution fusion | flops 1912995840 | bytes 10289152 | tf_op jit(solution)/shard_map/dot_general | solution.py:89
  161.8 0.0 all-reduce.11.cloned.1.call-update
  161.9 0.1 copy.14
  162.0 144.0 %all-reduce.11.cloned.1.call-done = f32[2432,384]{0,1:T(8,128)} async-done(((f32[2432,384]{0,1:T(8,128)}), f32[2432,384]{0,1:T(8,128)}) %all-reduce.11.cloned.1.call-update) | async-done | bytes 3735568
  306.0 1.1 dynamic-slice_add_fusion
  307.1 0.8 copy.15
  (18 shorter events, 0.1 us)
Async XLA Ops:
  7.2 62.8 %all-gather.3.cloned.1.call-start = ((), (), s32[]{:S(2)}) async-start(), calls=%async_computation | async-start | bytes 2027520 | tf_op jit(solution)/shard_map/all_gather | solution.py:53
  7.9 298.1 %all-reduce.11.cloned.1.call-start = ((), (), s32[]{:S(2)}) async-start(), calls=%async_computation.1 | async-start | bytes 7471104
  8.8 73.1 %collective-permute-start.4 = (f32[2,9,64]{2,1,0:T(8,128)S(1)}, f32[2,9,64]{2,1,0:T(8,128)S(1)}, u32[]{:S(2)}, u32[]{:S(2)}) collective-permute-start(f32[2,9,64]{2,1,0:T(8,128)S(1)} %get-tuple-element.29), channel_id=1, source_target_pairs={{0,8},{8,16},{16,24},{1,9},{9,17},{17,25},{2,10},{10,18},{18,26},{... | collective-permute-start | bytes 13832 | tf_op jit(solution)/shard_map/ppermute | solution.py:14
  13.7 68.2 %collective-permute-start.5 = (f32[2,9,64]{2,1,0:T(8,128)S(1)}, f32[2,9,64]{2,1,0:T(8,128)S(1)}, u32[]{:S(2)}, u32[]{:S(2)}) collective-permute-start(f32[2,9,64]{2,1,0:T(8,128)S(1)} %get-tuple-element.30), channel_id=1, source_target_pairs={{8,0},{16,8},{24,16},{9,1},{17,9},{25,17},{10,2},{18,10},{26,18},{... | collective-permute-start | bytes 13832 | tf_op jit(solution)/shard_map/ppermute | solution.py:17
  77.2 20.4 %collective-permute-start = (f32[8,64,384]{2,1,0:T(8,128)S(1)}, f32[8,64,384]{2,1,0:T(8,128)S(1)}, u32[]{:S(2)}, u32[]{:S(2)}) collective-permute-start(f32[8,64,384]{2,1,0:T(8,128)S(1)} %bitcast.43), channel_id=1, source_target_pairs={{0,8},{8,16},{16,24},{1,9},{9,17},{17,25},{2,10},{10,18},{18,26},{... | collective-permute-start | bytes 2359304 | tf_op jit(solution)/shard_map/ppermute | solution.py:14
  80.5 36.0 %collective-permute-start.1 = (f32[8,64,384]{2,1,0:T(8,128)S(1)}, f32[8,64,384]{2,1,0:T(8,128)S(1)}, u32[]{:S(2)}, u32[]{:S(2)}) collective-permute-start(f32[8,64,384]{2,1,0:T(8,128)S(1)} %bitcast.42), channel_id=1, source_target_pairs={{8,0},{16,8},{24,16},{9,1},{17,9},{25,17},{10,2},{18,10},{26,18},{... | collective-permute-start | bytes 2359304 | tf_op jit(solution)/shard_map/ppermute | solution.py:17
  82.0 3.3 %collective-permute-start.6 = (f32[2,34,9]{2,1,0:T(8,128)S(1)}, f32[2,34,9]{2,1,0:T(8,128)S(1)}, u32[]{:S(2)}, u32[]{:S(2)}) collective-permute-start(f32[2,34,9]{2,1,0:T(8,128)S(1)} %get-tuple-element.27), channel_id=1, source_target_pairs={{0,1},{1,2},{2,3},{3,4},{4,5},{5,6},{6,7},{8,9},{9,10},{10,11},{11... | collective-permute-start | bytes 7352 | tf_op jit(solution)/shard_map/ppermute | solution.py:14
  83.8 3.3 %collective-permute-start.7 = (f32[2,34,9]{2,1,0:T(8,128)S(1)}, f32[2,34,9]{2,1,0:T(8,128)S(1)}, u32[]{:S(2)}, u32[]{:S(2)}) collective-permute-start(f32[2,34,9]{2,1,0:T(8,128)S(1)} %get-tuple-element.28), channel_id=1, source_target_pairs={{1,0},{2,1},{3,2},{4,3},{5,4},{6,5},{7,6},{9,8},{10,9},{11,10},{12... | collective-permute-start | bytes 7352 | tf_op jit(solution)/shard_map/ppermute | solution.py:17
  116.6 3.0 collective-permute-start.2
  117.9 4.3 %collective-permute-start.3 = (f32[32,8,384]{2,1,0:T(8,128)S(1)}, f32[32,8,384]{2,1,0:T(8,128)S(1)}, u32[]{:S(2)}, u32[]{:S(2)}) collective-permute-start(f32[32,8,384]{2,1,0:T(8,128)S(1)} %get-tuple-element.24), channel_id=1, source_target_pairs={{1,0},{2,1},{3,2},{4,3},{5,4},{6,5},{7,6},{9,8},{10,9},{11,10},{12... | collective-permute-start | bytes 1179656 | tf_op jit(solution)/shard_map/ppermute | solution.py:17
  146.2 11.4 %slice-start = ((s8[4980736]{0:T(1024)(128)(4,1)}), s8[4194304]{0:T(1024)(128)(4,1)S(1)}, s32[]{:S(2)}) async-start(s8[4980736]{0:T(1024)(128)(4,1)} %bitcast.40), calls=%async_computation.2 | async-start | bytes 8388608
  150.0 7.6 %slice-start.1 = ((s8[4980736]{0:T(1024)(128)(4,1)}), s8[786432]{0:T(1024)(128)(4,1)S(1)}, s32[]{:S(2)}) async-start(s8[4980736]{0:T(1024)(128)(4,1)} %bitcast.40), calls=%async_computation.3 | async-start | bytes 1572864
  157.6 4.2 %copy-start = (f32[16,64,384]{2,1,0:T(8,128)}, f32[16,64,384]{2,1,0:T(8,128)S(1)}, u32[]{:S(2)}) copy-start(f32[16,64,384]{2,1,0:T(8,128)S(1)} %fusion.73) | copy-start | bytes 4718596
  157.6 4.2 %copy-start.1 = (bf16[76,384]{1,0:T(8,128)(2,1)S(1)}, bf16[76,384]{1,0:T(8,128)(2,1)}, u32[]{:S(2)}) copy-start(bf16[76,384]{1,0:T(8,128)(2,1)} %param.7) | copy-start | bytes 175108
  157.6 148.3 %copy-start.2 = (f32[76]{0:T(128)S(1)}, f32[76]{0:T(128)}, u32[]{:S(2)}) copy-start(f32[76]{0:T(128)} %param.8) | copy-start | bytes 916
Sparse Core Ops, SparseCore 0:
  11.0 58.9 all-gather.2
  162.0 143.9 all-reduce.10
where the time goes:
time: 315 us
  waiting for transfers between devices  233 us (74%)
  other arithmetic  37.6 us (12%)
  starting transfers between devices  16.6 us (5%)
  between operations  14.4 us (5%)
  matrix products  8.85 us (3%)
  local copies, waits for them, and re-layouts  3.95 us (1%)
    unnamed x3, waiting for transfers between devices  145 us
    all_gather x1, waiting for transfers between devices, local(): lax.all_gather(data_columns, ('gx', 'gy'), axis=0, tiled=True)  55 us
    mul x8, other arithmetic, local(): iterate = jacobi_step(extended, padded, weights, divisor) * retained  29.3 us
    ppermute x4, waiting for transfers between devices, padded_2(): lax.ppermute(lax.slice_in_dim(block, 0, width, axis=dim), axis, backward)  23.3 us
    ppermute x4, starting transfers between devices, padded_2(): lax.ppermute(lax.slice_in_dim(block, block.shape[dim] - width, None, axis...  11.3 us
    ppermute x4, waiting for transfers between devices, padded_2(): lax.ppermute(lax.slice_in_dim(block, block.shape[dim] - width, None, axis...  10.5 us
  transfers between devices with their start and end apart: 10, of which 6 were waited for; matrix products, arithmetic and copies ran while one was open for 3% of the time, Pallas kernels for 0%

commit v1 on v0

--- a/solution.py
+++ b/solution.py
@@ -1,9 +1,290 @@
+import functools
 import jax
 import jax.numpy as jnp
 from jax import lax
+from jax.experimental import pallas as pl
+from jax.experimental.pallas import tpu as pltpu
 from jax.sharding import PartitionSpec as P
 
 ITERS = 8
+MESH = pl.DeviceIdType.MESH
+
+
+def up8(n):
+    return -(-n // 8) * 8
+
+
+class Place:
+    def __init__(self, dims):
+        self.Y, self.X, self.Z = dims
+        gx, gy = lax.axis_index("gx"), lax.axis_index("gy")
+        self.y, self.x = gx // self.X, gx % self.X
+        self.z, self.core = gy // 2, gy % 2
+        self.n = {"x": self.X, "y": self.Y, "z": self.Z}
+        self.at = {"x": self.x, "y": self.y, "z": self.z}
+
+    def device(self, **moved):
+        c = {**self.at, "core": self.core, **moved}
+        return (c["y"] * self.X + c["x"], c["z"] * 2 + c["core"])
+
+    def ahead(self, axis, d):
+        return (self.at[axis] + d) % self.n[axis]
+
+    def peers(self):
+        found = [self.device(core=1 - self.core)]
+        for axis in "xyz":
+            found += [self.device(**{axis: self.ahead(axis, d)}) for d in range(1, self.n[axis])]
+        return found
+
+    def barrier(self):
+        ready = pltpu.get_barrier_semaphore()
+        peers = self.peers()
+        for peer in peers:
+            pl.semaphore_signal(ready, inc=1, device_id=peer, device_id_type=MESH)
+        pl.semaphore_wait(ready, len(peers))
+
+
+def remote(src, dst, send, recv, device):
+    return pltpu.make_async_remote_copy(
+        src_ref=src, dst_ref=dst, send_sem=send, recv_sem=recv, device_id=device, device_id_type=MESH
+    )
+
+
+def plane(ref, axis, index):
+    return ref.at[:, index] if axis == "x" else ref.at[index]
+
+
+def gather_kernel(dims, mine, full, own_sem, sz, rz, s1, r1, s2, r2, ss, rs):
+    here = Place(dims)
+    me = here.core
+    sib = here.device(core=1 - me)
+    home = full.at[here.y, here.x, here.z, me]
+    copy = pltpu.make_async_copy(mine, home, own_sem)
+    copy.start()
+    here.barrier()
+    copies = []
+    for d in range(1, here.Z):
+        sent = remote(mine, home, sz.at[d - 1], rz.at[d - 1], here.device(z=here.ahead("z", d)))
+        sent.start()
+        copies.append(sent)
+    copy.wait()
+    for d in range(1, here.Z):
+        back = full.at[here.y, here.x, here.ahead("z", -d), me]
+        remote(back, back, sz.at[d - 1], rz.at[d - 1], sib).wait_recv()
+    for c in (0, 1):
+
+        @pl.when(me == c)
+        def _():
+            near, far = "xy"[c], "yx"[c]
+            sent_here = []
+
+            def line(index, core):
+                where = {**here.at, near: index}
+                return full.at[where["y"], where["x"], :, core]
+
+            def sheet(index, core):
+                return full.at[index, :, :, core] if far == "y" else full.at[:, index, :, core]
+
+            own = line(here.at[near], c)
+            for d in range(1, here.n[near]):
+                sent = remote(
+                    own, own, s1.at[d - 1], r1.at[d - 1], here.device(**{near: here.ahead(near, d)})
+                )
+                sent.start()
+                sent_here.append(sent)
+            count = 0
+            share = remote(own, own, ss.at[count], rs.at[count], sib)
+            share.start()
+            sent_here.append(share)
+            for d in range(1, here.n[near]):
+                back = line(here.ahead(near, -d), c)
+                remote(back, back, s1.at[d - 1], r1.at[d - 1], sib).wait_recv()
+            own = sheet(here.at[far], c)
+            for d in range(1, here.n[far]):
+                sent = remote(
+                    own, own, s2.at[d - 1], r2.at[d - 1], here.device(**{far: here.ahead(far, d)})
+                )
+                sent.start()
+                sent_here.append(sent)
+            for d in range(1, here.n[near]):
+                count += 1
+                back = line(here.ahead(near, -d), c)
+                share = remote(back, back, ss.at[count], rs.at[count], sib)
+                share.start()
+                sent_here.append(share)
+            for d in range(1, here.n[far]):
+                back = sheet(here.ahead(far, -d), c)
+                remote(back, back, s2.at[d - 1], r2.at[d - 1], sib).wait_recv()
+                count += 1
+                share = remote(back, back, ss.at[count], rs.at[count], sib)
+                share.start()
+                sent_here.append(share)
+            near2, far2 = far, near
+            got = 0
+
+            def line2(index):
+                where = {**here.at, near2: index}
+                return full.at[where["y"], where["x"], :, 1 - c]
+
+            def sheet2(index):
+                return full.at[index, :, :, 1 - c] if far2 == "y" else full.at[:, index, :, 1 - c]
+
+            for d in range(0, here.n[near2]):
+                back = line2(here.ahead(near2, -d))
+                remote(back, back, ss.at[got], rs.at[got], sib).wait_recv()
+                got += 1
+            for d in range(1, here.n[far2]):
+                back = sheet2(here.ahead(far2, -d))
+                remote(back, back, ss.at[got], rs.at[got], sib).wait_recv()
+                got += 1
+            for sent in sent_here:
+                sent.wait_send()
+
+    for sent in copies:
+        sent.wait_send()
+
+
+def gather(dims, block):
+    Y, X, Z = dims
+    dma = pltpu.SemaphoreType.DMA
+    widest = max(X, Y)
+    return pl.pallas_call(
+        functools.partial(gather_kernel, dims),
+        out_shape=jax.ShapeDtypeStruct((Y, X, Z, 2) + block.shape, block.dtype),
+        in_specs=[pl.BlockSpec(memory_space=pltpu.VMEM)],
+        out_specs=pl.BlockSpec(memory_space=pltpu.VMEM),
+        scratch_shapes=[dma]
+        + [dma((max(Z - 1, 1),))] * 2
+        + [dma((widest,))] * 4
+        + [dma((X + Y,))] * 2,
+        compiler_params=pltpu.CompilerParams(
+            collective_id=0, has_side_effects=True, vmem_limit_bytes=16 << 20
+        ),
+    )(block)
+
+
+def scatter_kernel(dims, starts, H, part, out, total, r0, r1x, r1y, r2x, r2y, r3, *sems):
+    here = Place(dims)
+    me = here.core
+    sib = here.device(core=1 - me)
+    s0, g0, s1, g1, s2, g2, s3, g3 = sems
+    here.barrier()
+    for c in (0, 1):
+
+        @pl.when(me == c)
+        def _():
+            near, far = "xy"[c], "yx"[c]
+            r1, r2 = (r1x, r2y) if c == 0 else (r1y, r2x)
+            n1, n2 = here.n[near], here.n[far]
+            sent_here = []
+            for order, d in enumerate([*range(1, n2), 0]):
+                index = here.ahead(far, d)
+                sent = remote(
+                    plane(part, far, index).at[:, :, pl.ds(starts[1 - c], H), :],
+                    plane(r0, far, index),
+                    s0.at[order],
+                    g0.at[order],
+                    sib,
+                )
+                sent.start()
+                sent_here.append(sent)
+            for order, d in enumerate([*range(1, n1), 0]):
+                index = here.ahead(near, d)
+                arrived = plane(r0, near, index)
+                remote(arrived, arrived, s0.at[order], g0.at[order], sib).wait_recv()
+                held = plane(total, near, index)
+                held[...] = (
+                    plane(part, near, index).at[:, :, pl.ds(starts[c], H), :][...] + arrived[...]
+                )
+                if d:
+                    sent = remote(
+                        held, r1.at[d - 1], s1.at[d - 1], g1.at[d - 1], here.device(**{near: index})
+                    )
+                    sent.start()
+                    sent_here.append(sent)
+            for d in range(1, n1):
+                remote(r1.at[d - 1], r1.at[d - 1], s1.at[d - 1], g1.at[d - 1], sib).wait_recv()
+            mine = plane(total, near, here.at[near])
+            for d in [*range(1, n2), 0]:
+                index = here.ahead(far, d)
+                held = mine.at[index]
+                value = held[...]
+                for e in range(1, n1):
+                    value = value + r1.at[e - 1, index][...]
+                held[...] = value
+                if d:
+                    sent = remote(
+                        held, r2.at[d - 1], s2.at[d - 1], g2.at[d - 1], here.device(**{far: index})
+                    )
+                    sent.start()
+                    sent_here.append(sent)
+            for d in range(1, n2):
+                remote(r2.at[d - 1], r2.at[d - 1], s2.at[d - 1], g2.at[d - 1], sib).wait_recv()
+            for d in [*range(1, here.Z), 0]:
+                index = here.ahead("z", d)
+                held = total.at[here.y, here.x, index]
+                value = held[...]
+                for e in range(1, n2):
+                    value = value + r2.at[e - 1, index][...]
+                held[...] = value
+                if d:
+                    sent = remote(
+                        held, r3.at[d - 1], s3.at[d - 1], g3.at[d - 1], here.device(z=index)
+                    )
+                    sent.start()
+                    sent_here.append(sent)
+            value = total.at[here.y, here.x, here.z][...]
+            for d in range(1, here.Z):
+                remote(r3.at[d - 1], r3.at[d - 1], s3.at[d - 1], g3.at[d - 1], sib).wait_recv()
+                value = value + r3.at[d - 1][...]
+            out[...] = value
+            for sent in sent_here:
+                sent.wait_send()
+
+
+def scatter(dims, part, rows):
+    Y, X, Z = dims
+    columns = part.shape[1]
+    start = rows // 8 * 8
+    H = max(up8(rows), up8(2 * rows) - start)
+    pair = max(H + start, 2 * rows)
+    part = part.reshape(Y, X, Z, 2 * rows, columns)
+    if pair != 2 * rows:
+        part = jnp.pad(part, ((0, 0),) * 3 + ((0, pair - 2 * rows), (0, 0)))
+    dma = pltpu.SemaphoreType.DMA
+    widest = max(X, Y)
+    f32 = jnp.float32
+
+    def held(*lead):
+        return pltpu.VMEM(tuple(max(n, 1) for n in lead) + (H, columns), f32)
+
+    out = pl.pallas_call(
+        functools.partial(scatter_kernel, dims, (0, start), H),
+        out_shape=jax.ShapeDtypeStruct((H, columns), f32),
+        in_specs=[pl.BlockSpec(memory_space=pltpu.VMEM)],
+        out_specs=pl.BlockSpec(memory_space=pltpu.VMEM),
+        scratch_shapes=[
+            held(Y, X, Z),
+            held(Y, X, Z),
+            held(X - 1, Y, Z),
+            held(Y - 1, X, Z),
+            held(X - 1, Z),
+            held(Y - 1, Z),
+            held(Z - 1),
+        ]
+        + [dma((widest,))] * 6
+        + [dma((max(Z - 1, 1),))] * 2,
+        compiler_params=pltpu.CompilerParams(
+            collective_id=1, has_side_effects=True, vmem_limit_bytes=32 << 20
+        ),
+    )(part)
+    core = lax.axis_index("gy") % 2
+    return jnp.where(core == 0, out[:rows], out[rows - start : 2 * rows - start])
+
+
+def mesh_dims():
+    gx, gy = lax.axis_size("gx"), lax.axis_size("gy")
+    return (gx // 2, 2, gy // 2)
 
 
 def padded_2(block, sides, width):
@@ -50,7 +331,7 @@
     selected = flattened
     source = jnp.dot(
         selected,
-        lax.all_gather(data_columns, ("gx", "gy"), axis=0, tiled=True),
+        gather(mesh_dims(), data_columns).reshape(data_rows, columns_count),
         preferred_element_type=jnp.float32,
     )
     source = source.reshape(tile_rows, tile_cols, columns_count)
@@ -85,14 +366,10 @@
     iterate = iterate[margin : margin + tile_rows, margin : margin + tile_cols]
     smooth = iterate.astype(jnp.bfloat16).reshape(tile_rows * tile_cols, columns_count)
     selected = flattened
-    forward = lax.psum_scatter(
-        lax.dot_general(
-            selected, smooth, (((0,), (0,)), ((), ())), preferred_element_type=jnp.float32
-        ),
-        ("gx", "gy"),
-        scatter_dimension=0,
-        tiled=True,
-    )
+    partial = lax.dot_general(
+        selected, smooth, (((0,), (0,)), ((), ())), preferred_element_type=jnp.float32
+    )
+    forward = scatter(mesh_dims(), partial, data_columns.shape[0])
     return (forward + noise_var[:, None] * data_columns.astype(jnp.float32), iterate)
 
 

time: 315 us -> 178 us (0.57)
  waiting for transfers between devices: 233 us -> 16.5 us
  Pallas kernels: 0 us -> 83.7 us
  between operations: 14.4 us -> 0.96 us
  local copies, waits for them, and re-layouts: 3.95 us -> 11.5 us
    unnamed x3 -> x0, waiting for transfers between devices: 145 us -> none
    pallas_call x0 -> x2, Pallas kernels: none -> 83.7 us  [the longest x1 56.3 us: scatter(): pl.pallas_call(functools.partial(scatter_kernel, dims, (0, start), H), ou...]
    all_gather x1 -> x0, waiting for transfers between devices: 55 us -> none  [local(): lax.all_gather(data_columns, ('gx', 'gy'), axis=0, tiled=True)]
    ppermute x4, waiting for transfers between devices: 10.5 us -> 0.99 us  [padded_2(): lax.ppermute(lax.slice_in_dim(block, block.shape[dim] - width, None, axis...]
    ppermute x4, waiting for transfers between devices: 23.3 us -> 15.6 us  [padded_2(): lax.ppermute(lax.slice_in_dim(block, 0, width, axis=dim), axis, backward)]
    dot_general x0 -> x1, local copies, waits for them, and re-layouts: none -> 5.43 us  [local(): lax.dot_general(selected, smooth, (((0,), (0,)), ((), ())), preferred_ele...]
  transfers between devices with their start and end apart: 10 -> 8, of which waited for: 6 -> 4; matrix products, arithmetic and copies ran while one was open for 3% -> 5% of each run, Pallas kernels for 0% -> 15%
where the time goes in v1:
time: 178 us
  Pallas kernels  83.7 us (47%)
  other arithmetic  37.2 us (21%)
  starting transfers between devices  18.3 us (10%)
  waiting for transfers between devices  16.5 us (9%)
  local copies, waits for them, and re-layouts  11.5 us (6%)
  matrix products  9.33 us (5%)
    pallas_call x1, Pallas kernels, scatter(): pl.pallas_call(functools.partial(scatter_kernel, dims, (0, start), H), ou...  56.3 us
    mul x8, other arithmetic, local(): iterate = jacobi_step(extended, padded, weights, divisor) * retained  29.3 us
    pallas_call x1, Pallas kernels, gather(): pl.pallas_call(functools.partial(gather_kernel, dims), out_shape=jax.Shap...  27.3 us
    ppermute x4, waiting for transfers between devices, padded_2(): lax.ppermute(lax.slice_in_dim(block, 0, width, axis=dim), axis, backward)  15.6 us
    ppermute x4, starting transfers between devices, padded_2(): lax.ppermute(lax.slice_in_dim(block, block.shape[dim] - width, None, axis...  13.2 us
    dot_general x1, local copies, waits for them, and re-layouts, local(): lax.dot_general(selected, smooth, (((0,), (0,)), ((), ())), preferred_ele...  5.43 us
    dot_general x1, matrix products, local(): jnp.dot(selected, gather(mesh_dims(), data_columns).reshape(data_rows, co...  5.23 us
    ppermute x4, starting transfers between devices, padded_2(): lax.ppermute(lax.slice_in_dim(block, 0, width, axis=dim), axis, backward)  5.16 us
  transfers between devices with their start and end apart: 8, of which 4 were waited for; matrix products, arithmetic and copies ran while one was open for 5% of the time, Pallas kernels for 15%

profile of v1, /device:TPU:0, one launch (start us, length us, event | category | flops | bytes accessed | tf_op | source)
XLA Modules:
  0.0 177.5 jit_solution(9918907825701276427)
XLA Ops:
  0.6 0.8 select_reduce_fusion.1
  1.5 4.9 %collective-permute-start.4 = (f32[2,9,64]{2,1,0:T(8,128)S(1)}, f32[2,9,64]{2,1,0:T(8,128)S(1)}, u32[]{:S(2)}, u32[]{:S(2)}) collective-permute-start(f32[2,9,64]{2,1,0:T(8,128)S(1)} %get-tuple-element.21), channel_id=1, source_target_pairs={{0,8},{8,16},{16,24},{1,9},{9,17},{17,25},{2,10},{10,18},{18,26},{... | collective-permute-start | bytes 13832 | tf_op jit(solution)/shard_map/ppermute | solution.py:295
  6.4 1.3 collective-permute-start.5
  7.7 0.0 copy-start.1
  7.7 0.8 copy-done.1
  8.5 27.3 %shard_map.77 = bf16[2,2,4,2,76,384]{5,4,3,2,1,0:T(8,128)(2,1)S(1)} custom-call(bf16[76,384]{1,0:T(8,128)(2,1)S(1)} %copy-done.1), custom_call_target="tpu_custom_call" | custom-call | tf_op jit(solution)/shard_map/pallas_call | solution.py:151
  35.8 1.5 reshape.73
  37.3 5.2 %fusion.91 = f32[1024,384]{1,0:T(8,128)S(1)} fusion(bf16[1024,2432]{1,0:T(8,128)(2,1)} %bitcast.38, bf16[2432,384]{1,0:T(8,128)(2,1)} %reshape.73), kind=kOutput, calls=%fused_computation.147 | convolution fusion | flops 1912602624 | bytes 8421376 | tf_op jit(solution)/shard_map/dot_general | solution.py:332
  42.5 1.2 fusion.89
  43.8 1.3 collective-permute-start.1
  45.1 4.8 %collective-permute-start = (f32[8,64,384]{2,1,0:T(8,128)}, f32[8,64,384]{2,1,0:T(8,128)S(1)}, u32[]{:S(2)}, u32[]{:S(2)}) collective-permute-start(f32[8,64,384]{2,1,0:T(8,128)} %bitcast.1), channel_id=1, source_target_pairs={{0,8},{8,16},{16,24},{1,9},{9,17},{17,25},{2,10},{10,18},{18,26},{... | collective-permute-start | bytes 2359304 | tf_op jit(solution)/shard_map/ppermute | solution.py:295
  49.9 0.0 collective-permute-done.4
  50.0 0.1 fusion.90
  50.1 2.0 %collective-permute-start.6 = (f32[2,34,9]{2,1,0:T(8,128)S(1)}, f32[2,34,9]{2,1,0:T(8,128)S(1)}, u32[]{:S(2)}, u32[]{:S(2)}) collective-permute-start(f32[2,34,9]{2,1,0:T(8,128)S(1)} %get-tuple-element.19), channel_id=1, source_target_pairs={{0,1},{1,2},{2,3},{3,4},{4,5},{5,6},{6,7},{8,9},{9,10},{10,11},{11... | collective-permute-start | bytes 7352 | tf_op jit(solution)/shard_map/ppermute | solution.py:295
  52.1 1.3 collective-permute-start.7
  53.4 0.1 and_convert_fusion
  53.4 0.1 slice.229
  53.5 1.9 %collective-permute-done.7 = f32[2,34,9]{2,1,0:T(8,128)S(1)} collective-permute-done((f32[2,34,9]{2,1,0:T(8,128)S(1)}, f32[2,34,9]{2,1,0:T(8,128)S(1)}, u32[]{:S(2)}, u32[]{:S(2)}) %collective-permute-start.7) | collective-permute-done | bytes 2480 | tf_op jit(solution)/shard_map/ppermute | solution.py:298
  55.4 0.1 pad_maximum_fusion.5
  55.5 11.0 %collective-permute-done.1 = f32[8,64,384]{2,1,0:T(8,128)S(1)} collective-permute-done((f32[8,64,384]{2,1,0:T(8,128)}, f32[8,64,384]{2,1,0:T(8,128)S(1)}, u32[]{:S(2)}, u32[]{:S(2)}) %collective-permute-start.1) | collective-permute-done | bytes 786464 | tf_op jit(solution)/shard_map/ppermute | solution.py:298
  66.5 1.0 collective-permute-done
  67.5 0.1 pad_maximum_fusion.3
  67.6 1.5 collective-permute-start.2
  69.0 1.3 collective-permute-start.3
  70.3 0.1 and_select_fusion
  70.5 0.1 slice.222
  70.5 0.1 slice.224
  70.6 0.1 slice.226
  70.7 0.1 slice.228
  70.8 2.7 %collective-permute-done.3 = f32[32,8,384]{2,1,0:T(8,128)S(1)} collective-permute-done((f32[32,8,384]{2,1,0:T(8,128)S(1)}, f32[32,8,384]{2,1,0:T(8,128)S(1)}, u32[]{:S(2)}, u32[]{:S(2)}) %collective-permute-start.3) | collective-permute-done | bytes 393248 | tf_op jit(solution)/shard_map/ppermute | solution.py:298
  73.4 1.2 pad_maximum_fusion
  74.6 3.8 %fusion.70 = f32[32,80,384]{2,1,0:T(8,128)S(1)} fusion(f32[32,80,384]{2,1,0:T(8,128)S(1)} %get-tuple-element.10, f32[32,80]{1,0:T(8,128)S(1)} %get-tuple-element.8, f32[32,80]{1,0:T(8,128)S(1)} %get-tuple-element.7, f32[32,80]{1,0:T(8,128)S(1)} %get-tuple-element.6, f32[32,80]{1,0:T(8,128)S(1)} %and_convert_fusion, f32[32,80]{1,0:T(8,128)S(1)} %get-tuple-element.4, ...), kind=kLoop, calls=%fused_computation.105 | loop fusion | flops 13762560 | bytes 11857920 | tf_op jit(solution)/shard_map/mul | solution.py:365
  78.4 3.8 %fusion.69 = f32[32,80,384]{2,1,0:T(8,128)S(1)} fusion(f32[32,80,384]{2,1,0:T(8,128)S(1)} %fusion.70, f32[32,80]{1,0:T(8,128)S(1)} %get-tuple-element.8, f32[32,80]{1,0:T(8,128)S(1)} %get-tuple-element.7, f32[32,80]{1,0:T(8,128)S(1)} %get-tuple-element.6, f32[32,80]{1,0:T(8,128)S(1)} %and_convert_fusion, f32[32,80]{1,0:T(8,128)S(1)} %get-tuple-element.4, ...), kind=kLoop, calls=%fused_computation.104 | loop fusion | flops 13762560 | bytes 11857920 | tf_op jit(solution)/shard_map/mul | solution.py:365
  82.2 3.8 %fusion.68 = f32[32,80,384]{2,1,0:T(8,128)S(1)} fusion(f32[32,80,384]{2,1,0:T(8,128)S(1)} %fusion.69, f32[32,80]{1,0:T(8,128)S(1)} %get-tuple-element.8, f32[32,80]{1,0:T(8,128)S(1)} %get-tuple-element.7, f32[32,80]{1,0:T(8,128)S(1)} %get-tuple-element.6, f32[32,80]{1,0:T(8,128)S(1)} %and_convert_fusion, f32[32,80]{1,0:T(8,128)S(1)} %get-tuple-element.4, ...), kind=kLoop, calls=%fused_computation.103 | loop fusion | flops 13762560 | bytes 11857920 | tf_op jit(solution)/shard_map/mul | solution.py:365
  86.0 3.8 %fusion.67 = f32[32,80,384]{2,1,0:T(8,128)S(1)} fusion(f32[32,80,384]{2,1,0:T(8,128)S(1)} %fusion.68, f32[32,80]{1,0:T(8,128)S(1)} %get-tuple-element.8, f32[32,80]{1,0:T(8,128)S(1)} %get-tuple-element.7, f32[32,80]{1,0:T(8,128)S(1)} %get-tuple-element.6, f32[32,80]{1,0:T(8,128)S(1)} %and_convert_fusion, f32[32,80]{1,0:T(8,128)S(1)} %get-tuple-element.4, ...), kind=kLoop, calls=%fused_computation.102 | loop fusion | flops 13762560 | bytes 11857920 | tf_op jit(solution)/shard_map/mul | solution.py:365
  89.8 3.8 %fusion.66 = f32[32,80,384]{2,1,0:T(8,128)S(1)} fusion(f32[32,80,384]{2,1,0:T(8,128)S(1)} %fusion.67, f32[32,80]{1,0:T(8,128)S(1)} %get-tuple-element.8, f32[32,80]{1,0:T(8,128)S(1)} %get-tuple-element.7, f32[32,80]{1,0:T(8,128)S(1)} %get-tuple-element.6, f32[32,80]{1,0:T(8,128)S(1)} %and_convert_fusion, f32[32,80]{1,0:T(8,128)S(1)} %get-tuple-element.4, ...), kind=kLoop, calls=%fused_computation.101 | loop fusion | flops 13762560 | bytes 11857920 | tf_op jit(solution)/shard_map/mul | solution.py:365
  93.6 3.8 %fusion.65 = f32[32,80,384]{2,1,0:T(8,128)S(1)} fusion(f32[32,80,384]{2,1,0:T(8,128)S(1)} %fusion.66, f32[32,80]{1,0:T(8,128)S(1)} %get-tuple-element.8, f32[32,80]{1,0:T(8,128)S(1)} %get-tuple-element.7, f32[32,80]{1,0:T(8,128)S(1)} %get-tuple-element.6, f32[32,80]{1,0:T(8,128)S(1)} %and_convert_fusion, f32[32,80]{1,0:T(8,128)S(1)} %get-tuple-element.4, ...), kind=kLoop, calls=%fused_computation.100 | loop fusion | flops 13762560 | bytes 11857920 | tf_op jit(solution)/shard_map/mul | solution.py:365
  97.4 0.0 slice-start
  97.4 3.8 %fusion.64 = f32[32,80,384]{2,1,0:T(8,128)S(1)} fusion(f32[32,80,384]{2,1,0:T(8,128)S(1)} %fusion.65, f32[32,80]{1,0:T(8,128)S(1)} %get-tuple-element.8, f32[32,80]{1,0:T(8,128)S(1)} %get-tuple-element.7, f32[32,80]{1,0:T(8,128)S(1)} %get-tuple-element.6, f32[32,80]{1,0:T(8,128)S(1)} %and_convert_fusion, f32[32,80]{1,0:T(8,128)S(1)} %get-tuple-element.4, ...), kind=kLoop, calls=%fused_computation.99 | loop fusion | flops 13762560 | bytes 11857920 | tf_op jit(solution)/shard_map/mul | solution.py:365
  101.2 0.0 slice-start.1
  101.2 4.7 %fusion.63 = (f32[32,80,384]{2,1,0:T(8,128)S(1)}, f32[32,80,384]{2,1,0:T(8,128)}, f32[32,80,384]{2,1,0:T(8,128)}, f32[32,80,384]{2,1,0:T(8,128)}) fusion(f32[32,80,384]{2,1,0:T(8,128)S(1)} %fusion.64, f32[32,80]{1,0:T(8,128)S(1)} %get-tuple-element.5), kind=kLoop, calls=%fused_computation.96 | loop fusion | flops 983040 | bytes 19671040 | tf_op jit(solution)/shard_map/mul | solution.py:320
  106.0 2.8 %fusion.73 = f32[16,64,384]{2,1,0:T(8,128)S(1)} fusion(f32[32,80,384]{2,1,0:T(8,128)} %get-tuple-element.14, f32[32,80,384]{2,1,0:T(8,128)} %get-tuple-element.13, f32[32,80,384]{2,1,0:T(8,128)} %get-tuple-element.12, f32[32,80,384]{2,1,0:T(8,128)S(1)} %get-tuple-element.11, f32[32,80,384]{2,1,0:T(8,128)S(1)} %get-tuple-element.9, f32[16,64]{1,0:T(8,128)S(1)} %slice.229, ...), kind=kLoop, calls=%fused_computation.109 | loop fusion | flops 3538944 | bytes 9457664 | tf_op jit(solution)/shard_map/mul | solution.py:365
  108.8 0.0 copy-start.3
  108.8 4.1 %convolution_bitcast_fusion = f32[2432,384]{0,1:T(8,128)} fusion(bf16[16,64,2432]{2,1,0:T(8,128)(2,1)S(1)} %bitcast.40, f32[16,64,384]{2,1,0:T(8,128)S(1)} %fusion.73), kind=kOutput, calls=%fused_computation.32 | convolution fusion | flops 1912995840 | bytes 10289152 | tf_op jit(solution)/shard_map/dot_general | solution.py:369
  112.9 5.4 %copy.10 = f32[2432,384]{1,0:T(8,128)} copy(f32[2432,384]{0,1:T(8,128)} %convolution_bitcast_fusion) | data formatting | bytes 7471104 | tf_op jit(solution)/shard_map/dot_general | solution.py:369
  118.4 2.1 %copy-done = f32[2432,384]{1,0:T(8,128)S(1)} copy-done((f32[2432,384]{1,0:T(8,128)S(1)}, f32[2432,384]{1,0:T(8,128)}, u32[]{:S(2)}) %copy-start) | copy-done | bytes 3735576
  120.4 56.3 %shard_map.78 = f32[80,384]{1,0:T(8,128)S(1)} custom-call(f32[2,2,4,152,384]{4,3,2,1,0:T(8,128)S(1)} %bitcast.28), custom_call_target="tpu_custom_call" | custom-call | tf_op jit(solution)/shard_map/pallas_call | solution.py:261
  176.8 0.7 multiply_add_fusion
  (17 shorter events, 0.1 us)
Async XLA Ops:
  1.5 48.5 %collective-permute-start.4 = (f32[2,9,64]{2,1,0:T(8,128)S(1)}, f32[2,9,64]{2,1,0:T(8,128)S(1)}, u32[]{:S(2)}, u32[]{:S(2)}) collective-permute-start(f32[2,9,64]{2,1,0:T(8,128)S(1)} %get-tuple-element.21), channel_id=1, source_target_pairs={{0,8},{8,16},{16,24},{1,9},{9,17},{17,25},{2,10},{10,18},{18,26},{... | collective-permute-start | bytes 13832 | tf_op jit(solution)/shard_map/ppermute | solution.py:295
  6.4 43.6 %collective-permute-start.5 = (f32[2,9,64]{2,1,0:T(8,128)S(1)}, f32[2,9,64]{2,1,0:T(8,128)S(1)}, u32[]{:S(2)}, u32[]{:S(2)}) collective-permute-start(f32[2,9,64]{2,1,0:T(8,128)S(1)} %get-tuple-element.22), channel_id=1, source_target_pairs={{8,0},{16,8},{24,16},{9,1},{17,9},{25,17},{10,2},{18,10},{26,18},{... | collective-permute-start | bytes 13832 | tf_op jit(solution)/shard_map/ppermute | solution.py:298
  7.7 0.8 copy-start.1
  43.8 22.8 %collective-permute-start.1 = (f32[8,64,384]{2,1,0:T(8,128)}, f32[8,64,384]{2,1,0:T(8,128)S(1)}, u32[]{:S(2)}, u32[]{:S(2)}) collective-permute-start(f32[8,64,384]{2,1,0:T(8,128)} %bitcast.3), channel_id=1, source_target_pairs={{8,0},{16,8},{24,16},{9,1},{17,9},{25,17},{10,2},{18,10},{26,18},{... | collective-permute-start | bytes 2359304 | tf_op jit(solution)/shard_map/ppermute | solution.py:298
  45.1 22.5 %collective-permute-start = (f32[8,64,384]{2,1,0:T(8,128)}, f32[8,64,384]{2,1,0:T(8,128)S(1)}, u32[]{:S(2)}, u32[]{:S(2)}) collective-permute-start(f32[8,64,384]{2,1,0:T(8,128)} %bitcast.1), channel_id=1, source_target_pairs={{0,8},{8,16},{16,24},{1,9},{9,17},{17,25},{2,10},{10,18},{18,26},{... | collective-permute-start | bytes 2359304 | tf_op jit(solution)/shard_map/ppermute | solution.py:295
  50.1 3.5 %collective-permute-start.6 = (f32[2,34,9]{2,1,0:T(8,128)S(1)}, f32[2,34,9]{2,1,0:T(8,128)S(1)}, u32[]{:S(2)}, u32[]{:S(2)}) collective-permute-start(f32[2,34,9]{2,1,0:T(8,128)S(1)} %get-tuple-element.19), channel_id=1, source_target_pairs={{0,1},{1,2},{2,3},{3,4},{4,5},{5,6},{6,7},{8,9},{9,10},{10,11},{11... | collective-permute-start | bytes 7352 | tf_op jit(solution)/shard_map/ppermute | solution.py:295
  52.1 3.3 %collective-permute-start.7 = (f32[2,34,9]{2,1,0:T(8,128)S(1)}, f32[2,34,9]{2,1,0:T(8,128)S(1)}, u32[]{:S(2)}, u32[]{:S(2)}) collective-permute-start(f32[2,34,9]{2,1,0:T(8,128)S(1)} %get-tuple-element.20), channel_id=1, source_target_pairs={{1,0},{2,1},{3,2},{4,3},{5,4},{6,5},{7,6},{9,8},{10,9},{11,10},{12... | collective-permute-start | bytes 7352 | tf_op jit(solution)/shard_map/ppermute | solution.py:298
  67.6 3.2 %collective-permute-start.2 = (f32[32,8,384]{2,1,0:T(8,128)S(1)}, f32[32,8,384]{2,1,0:T(8,128)S(1)}, u32[]{:S(2)}, u32[]{:S(2)}) collective-permute-start(f32[32,8,384]{2,1,0:T(8,128)S(1)} %get-tuple-element.15), channel_id=1, source_target_pairs={{0,1},{1,2},{2,3},{3,4},{4,5},{5,6},{6,7},{8,9},{9,10},{10,11},{11... | collective-permute-start | bytes 1179656 | tf_op jit(solution)/shard_map/ppermute | solution.py:295
  69.0 4.4 %collective-permute-start.3 = (f32[32,8,384]{2,1,0:T(8,128)S(1)}, f32[32,8,384]{2,1,0:T(8,128)S(1)}, u32[]{:S(2)}, u32[]{:S(2)}) collective-permute-start(f32[32,8,384]{2,1,0:T(8,128)S(1)} %get-tuple-element.16), channel_id=1, source_target_pairs={{1,0},{2,1},{3,2},{4,3},{5,4},{6,5},{7,6},{9,8},{10,9},{11,10},{12... | collective-permute-start | bytes 1179656 | tf_op jit(solution)/shard_map/ppermute | solution.py:298
  97.4 11.4 %slice-start = ((s8[4980736]{0:T(1024)(128)(4,1)}), s8[4194304]{0:T(1024)(128)(4,1)S(1)}, s32[]{:S(2)}) async-start(s8[4980736]{0:T(1024)(128)(4,1)} %bitcast.39), calls=%async_computation | async-start | bytes 8388608
  101.2 7.6 %slice-start.1 = ((s8[4980736]{0:T(1024)(128)(4,1)}), s8[786432]{0:T(1024)(128)(4,1)S(1)}, s32[]{:S(2)}) async-start(s8[4980736]{0:T(1024)(128)(4,1)} %bitcast.39), calls=%async_computation.1 | async-start | bytes 1572864
  108.8 4.1 %copy-start.3 = (f32[16,64,384]{2,1,0:T(8,128)}, f32[16,64,384]{2,1,0:T(8,128)S(1)}, u32[]{:S(2)}) copy-start(f32[16,64,384]{2,1,0:T(8,128)S(1)} %fusion.73) | copy-start | bytes 4718596
  112.9 63.8 %copy-start.2 = (bf16[76,384]{1,0:T(8,128)(2,1)S(1)}, bf16[76,384]{1,0:T(8,128)(2,1)}, u32[]{:S(2)}) copy-start(bf16[76,384]{1,0:T(8,128)(2,1)} %mine.1) | copy-start | bytes 175108
  112.9 63.8 %copy-start.4 = (f32[76]{0:T(128)S(1)}, f32[76]{0:T(128)}, u32[]{:S(2)}) copy-start(f32[76]{0:T(128)} %param.8) | copy-start | bytes 916
  118.4 2.1 %copy-start = (f32[2432,384]{1,0:T(8,128)S(1)}, f32[2432,384]{1,0:T(8,128)}, u32[]{:S(2)}) copy-start(f32[2432,384]{1,0:T(8,128)} %copy.10) | copy-start | bytes 11206660

commit v2 on v1

--- a/solution.py
+++ b/solution.py
@@ -282,22 +282,135 @@
     return jnp.where(core == 0, out[:rows], out[rows - start : 2 * rows - start])
 
 
+def smooth_kernel(
+    counts, start, coef, prior, smooth, s, u, v, up_out, down_out, up_in, down_in, local, send, recv
+):
+    rows, cols, width = start.shape
+    m = ITERS
+    gx, gy = lax.axis_index("gx"), lax.axis_index("gy")
+    count_x, count_y = counts
+    sides = {
+        "n": (gx > 0, (gx - 1, gy), gx < count_x - 1),
+        "s": (gx < count_x - 1, (gx + 1, gy), gx > 0),
+        "w": (gy > 0, (gx, gy - 1), gy < count_y - 1),
+        "e": (gy < count_y - 1, (gx, gy + 1), gy > 0),
+    }
+    inner_r, inner_c = pl.ds(m, rows), pl.ds(m, cols)
+    low, high_r, high_c = pl.ds(0, m), pl.ds(m + rows, m), pl.ds(m + cols, m)
+    home = pltpu.make_async_copy(start, s.at[inner_r, inner_c], local)
+    home.start()
+    for side, where in (("n", (low, slice(None))), ("s", (high_r, slice(None)))):
+
+        @pl.when(jnp.logical_not(sides[side][0]))
+        def _():
+            s[where] = jnp.zeros((m, cols + 2 * m, width), jnp.float32)
+
+    for side, where in (("w", low), ("e", high_c)):
+
+        @pl.when(jnp.logical_not(sides[side][0]))
+        def _():
+            s[:, where] = jnp.zeros((rows + 2 * m, m, width), jnp.float32)
+
+    ready = pltpu.get_barrier_semaphore()
+    for has, peer, _ in sides.values():
+
+        @pl.when(has)
+        def _():
+            pl.semaphore_signal(ready, inc=1, device_id=peer, device_id_type=MESH)
+
+    up_out[...] = start[1:m].astype(jnp.bfloat16)
+    down_out[...] = start[rows - m : rows - 1].astype(jnp.bfloat16)
+    pl.semaphore_wait(ready, sum(jnp.where(has, 1, 0) for has, _, _ in sides.values()))
+
+    first = (
+        (0, "n", start.at[pl.ds(0, 1)], s.at[pl.ds(m + rows, 1), inner_c]),
+        (1, "s", start.at[pl.ds(rows - 1, 1)], s.at[pl.ds(m - 1, 1), inner_c]),
+        (2, "n", up_out, up_in),
+        (3, "s", down_out, down_in),
+        (4, "w", start.at[:, pl.ds(0, m)], s.at[inner_r, high_c]),
+        (5, "e", start.at[:, pl.ds(cols - m, m)], s.at[inner_r, low]),
+    )
+    second = (
+        (6, "w", s.at[low, pl.ds(m, m)], s.at[low, high_c]),
+        (7, "w", s.at[high_r, pl.ds(m, m)], s.at[high_r, high_c]),
+        (8, "e", s.at[low, pl.ds(cols, m)], s.at[low, low]),
+        (9, "e", s.at[high_r, pl.ds(cols, m)], s.at[high_r, low]),
+    )
+
+    def each(group, what):
+        for number, side, src, dst in group:
+            has, peer, gets = sides[side]
+            copy = remote(src, dst, send.at[number], recv.at[number], peer)
+
+            @pl.when(gets if what == "wait_recv" else has)
+            def _():
+                getattr(copy, what)()
+
+    each(first, "start")
+    home.wait()
+    each(first, "wait_recv")
+
+    @pl.when(sides["s"][0])
+    def _():
+        s[pl.ds(m + rows + 1, m - 1), inner_c] = up_in[...].astype(jnp.float32)
+
+    @pl.when(sides["n"][0])
+    def _():
+        s[pl.ds(0, m - 1), inner_c] = down_in[...].astype(jnp.float32)
+
+    each(second, "start")
+    each(second, "wait_recv")
+    each(first, "wait_send")
+    each(second, "wait_send")
+
+    held = [s, u, v]
+    wide = cols + 2 * m
+    for step in range(1, ITERS + 1):
+        old = s if step == 1 else held[1 + step % 2]
+        new = held[1 + (step + 1) % 2]
+        last = step == ITERS
+
+        @pl.loop(step, rows + 2 * m - step)
+        def _(r):
+            for g in range(width // 128):
+                lanes = pl.ds(g * 128, 128)
+                centre = old[r, :, lanes]
+                value = s[r, :, lanes] + coef[0, r] * old[r - 1, :, lanes]
+                value = value + coef[1, r] * old[r + 1, :, lanes]
+                value = value + coef[2, r] * pltpu.roll(centre, 1, 0)
+                value = value + coef[3, r] * pltpu.roll(centre, wide - 1, 0)
+                if last:
+                    prior[r - m, :, lanes] = value[m : m + cols]
+                    smooth[r - m, :, lanes] = value[m : m + cols].astype(jnp.bfloat16)
+                else:
+                    new[r, :, lanes] = value
+
+
+def smoothed(start, coef):
+    rows, cols, width = start.shape
+    m = ITERS
+    whole = pltpu.VMEM((rows + 2 * m, cols + 2 * m, width), jnp.float32)
+    strip = pltpu.VMEM((m - 1, cols, width), jnp.bfloat16)
+    dma = pltpu.SemaphoreType.DMA
+    vmem = pl.BlockSpec(memory_space=pltpu.VMEM)
+    return pl.pallas_call(
+        functools.partial(smooth_kernel, (lax.axis_size("gx"), lax.axis_size("gy"))),
+        out_shape=(
+            jax.ShapeDtypeStruct(start.shape, jnp.float32),
+            jax.ShapeDtypeStruct(start.shape, jnp.bfloat16),
+        ),
+        in_specs=[vmem, vmem],
+        out_specs=(vmem, vmem),
+        scratch_shapes=[whole] * 3 + [strip] * 4 + [dma, dma((10,)), dma((10,))],
+        compiler_params=pltpu.CompilerParams(
+            collective_id=2, has_side_effects=True, vmem_limit_bytes=40 << 20
+        ),
+    )(start, coef)
+
+
 def mesh_dims():
     gx, gy = lax.axis_size("gx"), lax.axis_size("gy")
     return (gx // 2, 2, gy // 2)
-
-
-def padded_2(block, sides, width):
-    for axis, dim in sides:
-        count = lax.axis_size(axis)
-        forward = [(i, i + 1) for i in range(count - 1)]
-        backward = [(target, source) for source, target in forward]
-        low = lax.ppermute(
-            lax.slice_in_dim(block, block.shape[dim] - width, None, axis=dim), axis, forward
-        )
-        high = lax.ppermute(lax.slice_in_dim(block, 0, width, axis=dim), axis, backward)
-        block = jnp.concatenate([low, block, high], axis=dim)
-    return block
 
 
 def lookup(classes, entries):
@@ -316,60 +429,44 @@
     return (north_w, south_w, west_w, east_w)
 
 
-def jacobi_step(source, padded, weights, divisor):
-    summed = source + weights[0][..., None] * padded[:-2, 1:-1]
-    summed = summed + weights[1][..., None] * padded[2:, 1:-1]
-    summed = summed + weights[2][..., None] * padded[1:-1, :-2]
-    summed = summed + weights[3][..., None] * padded[1:-1, 2:]
-    return summed / divisor[..., None]
-
-
 def local(operator_t, data_columns, noise_var, class_map, diffusion_table, kappa_table):
     tile_rows, tile_cols, data_rows = operator_t.shape
-    columns_count = data_columns.shape[1]
+    count, width = data_columns.shape
+    gx_size, gy_size = lax.axis_size("gx"), lax.axis_size("gy")
     flattened = operator_t.reshape(tile_rows * tile_cols, data_rows)
-    selected = flattened
-    source = jnp.dot(
-        selected,
-        gather(mesh_dims(), data_columns).reshape(data_rows, columns_count),
+    points = tile_rows * tile_cols
+    extra = -(-points // width)
+    classes = jnp.pad(class_map.reshape(points).astype(jnp.bfloat16), (0, extra * width - points))
+    block = jnp.concatenate([data_columns, classes.reshape(extra, width)], axis=0)
+    full = gather(mesh_dims(), block)
+    data = full[..., :count, :].reshape(data_rows, width)
+    classes = full[..., count:, :].reshape(gx_size, gy_size, extra * width)[..., :points]
+    classes = classes.reshape(gx_size, gy_size, tile_rows, tile_cols).astype(jnp.int32)
+    classes = classes.transpose(0, 2, 1, 3).reshape(gx_size * tile_rows, gy_size * tile_cols)
+    edge = ITERS + 1
+    classes = jnp.pad(classes, edge, constant_values=-1)
+    window = lax.dynamic_slice(
+        classes,
+        (lax.axis_index("gx") * tile_rows, lax.axis_index("gy") * tile_cols),
+        (tile_rows + 2 * edge, tile_cols + 2 * edge),
+    )
+    inside = (window >= 0)[1:-1, 1:-1]
+    weights = edge_weights(lookup(window, diffusion_table))
+    reaction = lookup(window, kappa_table)[1:-1, 1:-1]
+    divisor = jnp.where(inside, reaction + weights[0] + weights[1] + weights[2] + weights[3], 1.0)
+    coef = jnp.stack([jnp.where(inside, w / divisor, 0.0) for w in weights])
+    coef = jnp.broadcast_to(coef[..., None], coef.shape + (128,))
+    source = jnp.dot(flattened, data, preferred_element_type=jnp.float32)
+    tile_divisor = divisor[ITERS:-ITERS, ITERS:-ITERS]
+    start = source.reshape(tile_rows, tile_cols, width) / tile_divisor[..., None]
+    iterate, smooth = smoothed(start, coef)
+    partial = lax.dot_general(
+        flattened,
+        smooth.reshape(points, width),
+        (((0,), (0,)), ((), ())),
         preferred_element_type=jnp.float32,
     )
-    source = source.reshape(tile_rows, tile_cols, columns_count)
-    diffusion = lookup(class_map, diffusion_table)
-    reaction = lookup(class_map, kappa_table)
-    margin = ITERS
-    stacked = padded_2(jnp.stack([diffusion, reaction]), (("gx", 1), ("gy", 2)), margin + 1)
-    weights = edge_weights(stacked[0])
-    reaction_ext = stacked[1, 1:-1, 1:-1]
-    extended = padded_2(source, (("gx", 0), ("gy", 1)), margin)
-    global_rows = (
-        lax.axis_index("gx") * tile_rows
-        + jnp.arange(tile_rows + 2 * margin, dtype=jnp.int32)
-        - margin
-    )
-    global_cols = (
-        lax.axis_index("gy") * tile_cols
-        + jnp.arange(tile_cols + 2 * margin, dtype=jnp.int32)
-        - margin
-    )
-    rows_inside = (global_rows >= 0) & (global_rows < tile_rows * lax.axis_size("gx"))
-    cols_inside = (global_cols >= 0) & (global_cols < tile_cols * lax.axis_size("gy"))
-    inside = rows_inside[:, None] & cols_inside[None, :]
-    divisor = jnp.where(
-        inside, reaction_ext + weights[0] + weights[1] + weights[2] + weights[3], 1.0
-    )
-    retained = inside.astype(jnp.float32)[..., None]
-    iterate = extended / divisor[..., None] * retained
-    for repeat in range(ITERS):
-        padded = jnp.pad(iterate, ((1, 1), (1, 1), (0, 0)))
-        iterate = jacobi_step(extended, padded, weights, divisor) * retained
-    iterate = iterate[margin : margin + tile_rows, margin : margin + tile_cols]
-    smooth = iterate.astype(jnp.bfloat16).reshape(tile_rows * tile_cols, columns_count)
-    selected = flattened
-    partial = lax.dot_general(
-        selected, smooth, (((0,), (0,)), ((), ())), preferred_element_type=jnp.float32
-    )
-    forward = scatter(mesh_dims(), partial, data_columns.shape[0])
+    forward = scatter(mesh_dims(), partial, count)
     return (forward + noise_var[:, None] * data_columns.astype(jnp.float32), iterate)
 
 

time: 178 us -> 125 us (0.70)
  other arithmetic: 37.2 us -> 3.01 us
  starting transfers between devices: 18.3 us -> 0 us
  waiting for transfers between devices: 16.5 us -> 0 us
  Pallas kernels: 83.7 us -> 98.9 us
    mul x9 -> x0, other arithmetic: 34.1 us -> none  [the longest x8 29.3 us: local(): iterate = jacobi_step(extended, padded, weights, divisor) * retained]
    pallas_call x0 -> x1, Pallas kernels: none -> 26.7 us  [smoothed(): pl.pallas_call(functools.partial(smooth_kernel, (lax.axis_size('gx'), lax...]
    ppermute x8 -> x0, starting transfers between devices: 18.3 us -> none  [the longest x4 13.2 us: padded_2(): lax.ppermute(lax.slice_in_dim(block, block.shape[dim] - width, None, axis...]
    ppermute x8 -> x0, waiting for transfers between devices: 16.5 us -> none  [the longest x4 15.6 us: padded_2(): lax.ppermute(lax.slice_in_dim(block, 0, width, axis=dim), axis, backward)]
    pallas_call x1, Pallas kernels: 56.3 us -> 44.4 us  [scatter(): pl.pallas_call(functools.partial(scatter_kernel, dims, (0, start), H), ou...]
    dot_general x1 -> x2, local copies, waits for them, and re-layouts: 5.43 us -> 5.88 us  [the longest x1 5.42 us: local(): lax.dot_general(flattened, smooth.reshape(points, width), (((0,), (0,)),...]
  transfers between devices with their start and end apart: 8 -> 0, of which waited for: 4 -> 0; matrix products, arithmetic and copies ran while one was open for 5% -> 0% of each run, Pallas kernels for 15% -> 0%
where the time goes in v2:
time: 125 us
  Pallas kernels  98.9 us (79%)
  local copies, waits for them, and re-layouts  12.7 us (10%)
  matrix products  9.27 us (7%)
  other arithmetic  3.01 us (2%)
    pallas_call x1, Pallas kernels, scatter(): pl.pallas_call(functools.partial(scatter_kernel, dims, (0, start), H), ou...  44.4 us
    pallas_call x1, Pallas kernels, gather(): pl.pallas_call(functools.partial(gather_kernel, dims), out_shape=jax.Shap...  27.9 us
    pallas_call x1, Pallas kernels, smoothed(): pl.pallas_call(functools.partial(smooth_kernel, (lax.axis_size('gx'), lax...  26.7 us
    dot_general x1, local copies, waits for them, and re-layouts, local(): lax.dot_general(flattened, smooth.reshape(points, width), (((0,), (0,)),...  5.42 us
    dot_general x1, matrix products, local(): source = jnp.dot(flattened, data, preferred_element_type=jnp.float32)  5.22 us
    dot_general x1, matrix products, local(): lax.dot_general(flattened, smooth.reshape(points, width), (((0,), (0,)),...  4.05 us
    unnamed x15, local copies, waits for them, and re-layouts  3.23 us

profile of v2, /device:TPU:0, one launch (start us, length us, event | category | flops | bytes accessed | tf_op | source)
XLA Modules:
  0.0 124.7 jit_solution(11781090214471493533)
XLA Ops:
  0.6 0.0 copy-start.3
  0.6 0.0 copy-start.2
  0.7 0.7 convert_element_type.17
  1.4 0.1 convert_element_type.18
  1.5 0.8 pad_maximum_fusion.1.mine
  2.3 27.9 %shard_map.77 = bf16[2,2,4,2,79,384]{5,4,3,2,1,0:T(8,128)(2,1)S(1)} custom-call(bf16[79,384]{1,0:T(8,128)(2,1)S(1)} %pad_maximum_fusion.1.mine), custom_call_target="tpu_custom_call" | custom-call | tf_op jit(solution)/shard_map/pallas_call | solution.py:151
  30.2 0.1 slice.40
  30.2 0.1 reshape.42
  30.3 0.1 convert_element_type.19
  30.5 0.1 reshape.43
  30.7 0.1 fusion.8
  30.8 0.0 copy-done.3
  30.8 0.0 copy-done.2
  30.8 0.2 select_reduce_fusion
  31.0 0.1 select_bitcast_fusion.3
  31.1 0.1 slice.60
  31.2 0.1 select_bitcast_fusion.2
  31.3 1.4 %reshape.39 = bf16[2432,384]{1,0:T(8,128)(2,1)} reshape(bf16[2,2,4,2,76,384]{5,4,3,2,1,0:T(8,128)(2,1)S(1)} %bitcast.28) | data formatting | bytes 3735552 | tf_op jit(solution)/shard_map/reshape | solution.py:442
  32.7 5.2 %convolution_bitcast_fusion.1 = f32[1024,384]{0,1:T(8,128)S(1)} fusion(bf16[2432,384]{1,0:T(8,128)(2,1)} %reshape.39, bf16[1024,2432]{1,0:T(8,128)(2,1)} %bitcast.29), kind=kOutput, calls=%fused_computation.1 | convolution fusion | flops 1912602624 | bytes 8421376 | tf_op jit(solution)/shard_map/dot_general | solution.py:459
  38.0 0.5 copy.14
  38.4 0.0 slice-start
  38.5 0.2 broadcast_divide_fusion.start
  38.7 0.0 slice-start.1
  38.7 1.5 %broadcast_in_dim.26.coef = f32[4,32,80,128]{3,2,1,0:T(8,128)S(1)} broadcast(f32[4,32,80]{2,1,0:T(8,128)S(1)} %pad_maximum_fusion), dimensions={0,1,2} | broadcast | bytes 5283840 | tf_op jit(solution)/shard_map/broadcast_in_dim | solution.py:458
  40.2 26.7 %shard_map.78 = (f32[16,64,384]{2,1,0:T(8,128)S(1)}, bf16[16,64,384]{2,1,0:T(8,128)(2,1)S(1)}) custom-call(f32[16,64,384]{2,1,0:T(8,128)S(1)} %broadcast_divide_fusion.start, f32[4,32,80,128]{3,2,1,0:T(8,128)S(1)} %broadcast_in_dim.26.coef), custom_call_target="tpu_custom_call" | custom-call | tf_op jit(solution)/shard_map/pallas_call | solution.py:396
  66.9 0.0 slice-done
  66.9 0.0 slice-done.1
  66.9 4.1 %convolution_bitcast_fusion = f32[2432,384]{0,1:T(8,128)} fusion(bf16[16,64,384]{2,1,0:T(8,128)(2,1)S(1)} %get-tuple-element.4, bf16[16,64,2432]{2,1,0:T(8,128)(2,1)S(1)} %bitcast.31), kind=kOutput, calls=%fused_computation | convolution fusion | flops 1912602624 | bytes 9502720 | tf_op jit(solution)/shard_map/dot_general | solution.py:463
  71.0 5.4 %copy.16 = f32[2432,384]{1,0:T(8,128)} copy(f32[2432,384]{0,1:T(8,128)} %convolution_bitcast_fusion) | data formatting | bytes 7471104 | tf_op jit(solution)/shard_map/dot_general | solution.py:463
  76.4 0.0 copy-start
  76.4 2.1 %copy-done = f32[2432,384]{1,0:T(8,128)S(1)} copy-done((f32[2432,384]{1,0:T(8,128)S(1)}, f32[2432,384]{1,0:T(8,128)}, u32[]{:S(2)}) %copy-start) | copy-done | bytes 3735576
  78.4 0.0 copy-start.1
  78.4 0.0 copy-start.4
  78.4 44.4 %shard_map.79 = f32[80,384]{1,0:T(8,128)S(1)} custom-call(f32[2,2,4,152,384]{4,3,2,1,0:T(8,128)S(1)} %bitcast.27), custom_call_target="tpu_custom_call" | custom-call | tf_op jit(solution)/shard_map/pallas_call | solution.py:261
  122.8 0.0 copy-done.1
  122.8 0.0 copy-done.4
  122.9 0.7 multiply_add_fusion
  123.6 1.1 copy.20
  (6 shorter events, 0.1 us)
Async XLA Ops:
  0.6 30.2 %copy-start.3 = (f32[16]{0:T(128)S(1)}, f32[16]{0:T(128)}, u32[]{:S(2)}) copy-start(f32[16]{0:T(128)} %param.11) | copy-start | bytes 196
  0.6 30.2 %copy-start.2 = (f32[16]{0:T(128)S(1)}, f32[16]{0:T(128)}, u32[]{:S(2)}) copy-start(f32[16]{0:T(128)} %param.10) | copy-start | bytes 196
  38.4 28.4 %slice-start = ((s8[4980736]{0:T(1024)(128)(4,1)}), s8[4194304]{0:T(1024)(128)(4,1)S(1)}, s32[]{:S(2)}) async-start(s8[4980736]{0:T(1024)(128)(4,1)} %bitcast.30), calls=%async_computation | async-start | bytes 8388608
  38.7 28.2 %slice-start.1 = ((s8[4980736]{0:T(1024)(128)(4,1)}), s8[786432]{0:T(1024)(128)(4,1)S(1)}, s32[]{:S(2)}) async-start(s8[4980736]{0:T(1024)(128)(4,1)} %bitcast.30), calls=%async_computation.1 | async-start | bytes 1572864
  76.4 2.1 %copy-start = (f32[2432,384]{1,0:T(8,128)S(1)}, f32[2432,384]{1,0:T(8,128)}, u32[]{:S(2)}) copy-start(f32[2432,384]{1,0:T(8,128)} %copy.16) | copy-start | bytes 11206660
  78.4 44.4 %copy-start.1 = (bf16[76,384]{1,0:T(8,128)(2,1)S(1)}, bf16[76,384]{1,0:T(8,128)(2,1)}, u32[]{:S(2)}) copy-start(bf16[76,384]{1,0:T(8,128)(2,1)} %param.7) | copy-start | bytes 175108
  78.4 44.4 %copy-start.4 = (f32[76]{0:T(128)S(1)}, f32[76]{0:T(128)}, u32[]{:S(2)}) copy-start(f32[76]{0:T(128)} %param.8) | copy-start | bytes 916

commit v3 on v2

--- a/solution.py
+++ b/solution.py
@@ -48,10 +48,6 @@
     return pltpu.make_async_remote_copy(
         src_ref=src, dst_ref=dst, send_sem=send, recv_sem=recv, device_id=device, device_id_type=MESH
     )
-
-
-def plane(ref, axis, index):
-    return ref.at[:, index] if axis == "x" else ref.at[index]
 
 
 def gather_kernel(dims, mine, full, own_sem, sz, rz, s1, r1, s2, r2, ss, rs):
@@ -163,12 +159,51 @@
     )(block)
 
 
-def scatter_kernel(dims, starts, H, part, out, total, r0, r1x, r1y, r2x, r2y, r3, *sems):
+def scatter_kernel(dims, starts, H, fused, *refs):
+    if fused:
+        operator, field, out, total, r0, r1x, r1y, r2x, r2y, r3, part, wide, *sems = refs
+    else:
+        part, out, total, r0, r1x, r1y, r2x, r2y, r3, *sems = refs
     here = Place(dims)
+    Y, X, Z = dims
+    pair = part.shape[3]
     me = here.core
     sib = here.device(core=1 - me)
     s0, g0, s1, g1, s2, g2, s3, g3 = sems
-    here.barrier()
+    ready = pltpu.get_barrier_semaphore()
+    peers = here.peers()
+    for peer in peers:
+        pl.semaphore_signal(ready, inc=1, device_id=peer, device_id_type=MESH)
+    order = [(dy, dx) for dy in [*range(1, Y), 0] for dx in [*range(1, X), 0]]
+    order.sort(key=lambda step: (step[0] == 0) + (step[1] == 0))
+    for number, (dy, dx) in enumerate(order):
+        y, x = here.ahead("y", dy), here.ahead("x", dx)
+        if fused:
+            span = wide.shape[0]
+            row = (y * X + x) * (Z * pair)
+            base = jnp.minimum(row // 128, (operator.shape[1] - span) // 128) * 128
+            wide[...] = lax.dot_general(
+                operator[:, pl.ds(pl.multiple_of(base, 128), span)],
+                field[...],
+                (((0,), (0,)), ((), ())),
+                preferred_element_type=jnp.float32,
+            )
+            for z in range(Z):
+                part[y, x, z] = wide[pl.ds(pl.multiple_of(row - base + z * pair, 8), pair), :]
+        if number == 0:
+            pl.semaphore_wait(ready, len(peers))
+        for c in (0, 1):
+
+            @pl.when(me == c)
+            def _():
+                remote(
+                    part.at[y, x, :, pl.ds(starts[1 - c], H), :],
+                    r0.at[y, x],
+                    s0.at[number],
+                    g0.at[number],
+                    sib,
+                ).start()
+
     for c in (0, 1):
 
         @pl.when(me == c)
@@ -177,50 +212,46 @@
             r1, r2 = (r1x, r2y) if c == 0 else (r1y, r2x)
             n1, n2 = here.n[near], here.n[far]
             sent_here = []
-            for order, d in enumerate([*range(1, n2), 0]):
-                index = here.ahead(far, d)
-                sent = remote(
-                    plane(part, far, index).at[:, :, pl.ds(starts[1 - c], H), :],
-                    plane(r0, far, index),
-                    s0.at[order],
-                    g0.at[order],
-                    sib,
-                )
-                sent.start()
-                sent_here.append(sent)
-            for order, d in enumerate([*range(1, n1), 0]):
-                index = here.ahead(near, d)
-                arrived = plane(r0, near, index)
-                remote(arrived, arrived, s0.at[order], g0.at[order], sib).wait_recv()
-                held = plane(total, near, index)
-                held[...] = (
-                    plane(part, near, index).at[:, :, pl.ds(starts[c], H), :][...] + arrived[...]
-                )
+            sorted_steps = sorted(
+                enumerate(order), key=lambda item: (item[1][1 - c] == 0, item[0])
+            )
+            for number, (dy, dx) in sorted_steps:
+                y, x = here.ahead("y", dy), here.ahead("x", dx)
+                arrived = r0.at[y, x]
+                remote(arrived, arrived, s0.at[number], g0.at[number], sib).wait_recv()
+                held = total.at[y, x]
+                held[...] = part[y, x, :, pl.ds(starts[c], H), :] + arrived[...]
+                d = (dx, dy)[c]
                 if d:
                     sent = remote(
-                        held, r1.at[d - 1], s1.at[d - 1], g1.at[d - 1], here.device(**{near: index})
+                        held,
+                        r1.at[d - 1, (y, x)[c]],
+                        s1.at[number],
+                        g1.at[number],
+                        here.device(**{near: (x, y)[c]}),
                     )
                     sent.start()
                     sent_here.append(sent)
-            for d in range(1, n1):
-                remote(r1.at[d - 1], r1.at[d - 1], s1.at[d - 1], g1.at[d - 1], sib).wait_recv()
-            mine = plane(total, near, here.at[near])
-            for d in [*range(1, n2), 0]:
-                index = here.ahead(far, d)
-                held = mine.at[index]
+            for d2 in [*range(1, n2), 0]:
+                index = here.ahead(far, d2)
+                held = total.at[(index, here.x) if c == 0 else (here.y, index)]
                 value = held[...]
-                for e in range(1, n1):
-                    value = value + r1.at[e - 1, index][...]
+                for d in range(1, n1):
+                    number = order.index((d2, d) if c == 0 else (d, d2))
+                    back = r1.at[d - 1, index]
+                    remote(back, back, s1.at[number], g1.at[number], sib).wait_recv()
+                    value = value + back[...]
                 held[...] = value
-                if d:
+                if d2:
                     sent = remote(
-                        held, r2.at[d - 1], s2.at[d - 1], g2.at[d - 1], here.device(**{far: index})
+                        held, r2.at[d2 - 1], s2.at[d2 - 1], g2.at[d2 - 1],
+                        here.device(**{far: index}),
                     )
                     sent.start()
                     sent_here.append(sent)
             for d in range(1, n2):
                 remote(r2.at[d - 1], r2.at[d - 1], s2.at[d - 1], g2.at[d - 1], sib).wait_recv()
-            for d in [*range(1, here.Z), 0]:
+            for d in [*range(1, Z), 0]:
                 index = here.ahead("z", d)
                 held = total.at[here.y, here.x, index]
                 value = held[...]
@@ -234,23 +265,33 @@
                     sent.start()
                     sent_here.append(sent)
             value = total.at[here.y, here.x, here.z][...]
-            for d in range(1, here.Z):
+            for d in range(1, Z):
                 remote(r3.at[d - 1], r3.at[d - 1], s3.at[d - 1], g3.at[d - 1], sib).wait_recv()
                 value = value + r3.at[d - 1][...]
             out[...] = value
             for sent in sent_here:
                 sent.wait_send()
-
-
-def scatter(dims, part, rows):
+            for number, (dy, dx) in enumerate(order):
+                y, x = here.ahead("y", dy), here.ahead("x", dx)
+                remote(
+                    part.at[y, x, :, pl.ds(starts[1 - c], H), :],
+                    r0.at[y, x],
+                    s0.at[number],
+                    g0.at[number],
+                    sib,
+                ).wait_send()
+
+
+def scatter(dims, operator, field, rows):
     Y, X, Z = dims
-    columns = part.shape[1]
+    points, data_rows = operator.shape
+    columns = field.shape[1]
     start = rows // 8 * 8
     H = max(up8(rows), up8(2 * rows) - start)
     pair = max(H + start, 2 * rows)
-    part = part.reshape(Y, X, Z, 2 * rows, columns)
-    if pair != 2 * rows:
-        part = jnp.pad(part, ((0, 0),) * 3 + ((0, pair - 2 * rows), (0, 0)))
+    group = Z * pair
+    span = -(-(group + 127) // 128) * 128
+    fused = pair == 2 * rows and pair % 8 == 0 and data_rows % 128 == 0 and span <= data_rows
     dma = pltpu.SemaphoreType.DMA
     widest = max(X, Y)
     f32 = jnp.float32
@@ -258,26 +299,37 @@
     def held(*lead):
         return pltpu.VMEM(tuple(max(n, 1) for n in lead) + (H, columns), f32)
 
+    scratch = [
+        held(Y, X, Z),
+        held(Y, X, Z),
+        held(X - 1, Y, Z),
+        held(Y - 1, X, Z),
+        held(X - 1, Z),
+        held(Y - 1, Z),
+        held(Z - 1),
+    ]
+    if fused:
+        given = (operator, field)
+        scratch += [pltpu.VMEM((Y, X, Z, pair, columns), f32), pltpu.VMEM((span, columns), f32)]
+    else:
+        part = lax.dot_general(
+            operator, field, (((0,), (0,)), ((), ())), preferred_element_type=f32
+        ).reshape(Y, X, Z, 2 * rows, columns)
+        given = (jnp.pad(part, ((0, 0),) * 3 + ((0, pair - 2 * rows), (0, 0))),)
+    vmem = pl.BlockSpec(memory_space=pltpu.VMEM)
     out = pl.pallas_call(
-        functools.partial(scatter_kernel, dims, (0, start), H),
+        functools.partial(scatter_kernel, dims, (0, start), H, fused),
         out_shape=jax.ShapeDtypeStruct((H, columns), f32),
-        in_specs=[pl.BlockSpec(memory_space=pltpu.VMEM)],
-        out_specs=pl.BlockSpec(memory_space=pltpu.VMEM),
-        scratch_shapes=[
-            held(Y, X, Z),
-            held(Y, X, Z),
-            held(X - 1, Y, Z),
-            held(Y - 1, X, Z),
-            held(X - 1, Z),
-            held(Y - 1, Z),
-            held(Z - 1),
-        ]
-        + [dma((widest,))] * 6
+        in_specs=[vmem] * len(given),
+        out_specs=vmem,
+        scratch_shapes=scratch
+        + [dma((X * Y,))] * 4
+        + [dma((widest,))] * 2
         + [dma((max(Z - 1, 1),))] * 2,
         compiler_params=pltpu.CompilerParams(
-            collective_id=1, has_side_effects=True, vmem_limit_bytes=32 << 20
+            collective_id=1, has_side_effects=True, vmem_limit_bytes=40 << 20
         ),
-    )(part)
+    )(*given)
     core = lax.axis_index("gy") % 2
     return jnp.where(core == 0, out[:rows], out[rows - start : 2 * rows - start])
 
@@ -460,13 +512,7 @@
     tile_divisor = divisor[ITERS:-ITERS, ITERS:-ITERS]
     start = source.reshape(tile_rows, tile_cols, width) / tile_divisor[..., None]
     iterate, smooth = smoothed(start, coef)
-    partial = lax.dot_general(
-        flattened,
-        smooth.reshape(points, width),
-        (((0,), (0,)), ((), ())),
-        preferred_element_type=jnp.float32,
-    )
-    forward = scatter(mesh_dims(), partial, count)
+    forward = scatter(mesh_dims(), flattened, smooth.reshape(points, width), count)
     return (forward + noise_var[:, None] * data_columns.astype(jnp.float32), iterate)
 
 

time: 125 us -> 113 us (0.904)
  local copies, waits for them, and re-layouts: 12.7 us -> 5.23 us
  matrix products: 9.27 us -> 5.22 us
    dot_general x1 -> x0, local copies, waits for them, and re-layouts: 5.42 us -> none  [local(): lax.dot_general(flattened, smooth.reshape(points, width), (((0,), (0,)),...]
    dot_general x1 -> x0, matrix products: 4.05 us -> none  [local(): lax.dot_general(flattened, smooth.reshape(points, width), (((0,), (0,)),...]
    unnamed x15 -> x13, local copies, waits for them, and re-layouts: 3.23 us -> 1.18 us
where the time goes in v3:
time: 113 us
  Pallas kernels  98.3 us (87%)
  local copies, waits for them, and re-layouts  5.23 us (5%)
  matrix products  5.22 us (5%)
  other arithmetic  3.01 us (3%)
    pallas_call x1, Pallas kernels, scatter(): pl.pallas_call(functools.partial(scatter_kernel, dims, (0, start), H, fus...  43.8 us
    pallas_call x1, Pallas kernels, gather(): pl.pallas_call(functools.partial(gather_kernel, dims), out_shape=jax.Shap...  27.9 us
    pallas_call x1, Pallas kernels, smoothed(): pl.pallas_call(functools.partial(smooth_kernel, (lax.axis_size('gx'), lax...  26.7 us
    dot_general x1, matrix products, local(): source = jnp.dot(flattened, data, preferred_element_type=jnp.float32)  5.22 us

profile of v3, /device:TPU:0, one launch (start us, length us, event | category | flops | bytes accessed | tf_op | source)
XLA Modules:
  0.0 112.6 jit_solution(6169667552897680817)
XLA Ops:
  0.6 0.0 copy-start.2
  0.6 0.0 copy-start.1
  0.7 0.7 convert_element_type.17
  1.4 0.1 convert_element_type.18
  1.5 0.8 pad_maximum_fusion.1.mine
  2.3 27.9 %shard_map.77 = bf16[2,2,4,2,79,384]{5,4,3,2,1,0:T(8,128)(2,1)S(1)} custom-call(bf16[79,384]{1,0:T(8,128)(2,1)S(1)} %pad_maximum_fusion.1.mine), custom_call_target="tpu_custom_call" | custom-call | tf_op jit(solution)/shard_map/pallas_call | solution.py:147
  30.2 0.1 slice.40
  30.2 0.1 reshape.41
  30.3 0.1 convert_element_type.19
  30.5 0.1 reshape.42
  30.7 0.1 fusion.8
  30.8 0.0 copy-done.2
  30.8 0.0 copy-done.1
  30.8 0.2 select_reduce_fusion
  31.0 0.1 select_bitcast_fusion.3
  31.1 0.1 slice.60
  31.2 0.1 select_bitcast_fusion.2
  31.3 1.4 %reshape.39 = bf16[2432,384]{1,0:T(8,128)(2,1)} reshape(bf16[2,2,4,2,76,384]{5,4,3,2,1,0:T(8,128)(2,1)S(1)} %bitcast.21) | data formatting | bytes 3735552 | tf_op jit(solution)/shard_map/reshape | solution.py:494
  32.7 5.2 %convolution_bitcast_fusion = f32[1024,384]{0,1:T(8,128)S(1)} fusion(bf16[2432,384]{1,0:T(8,128)(2,1)} %reshape.39, bf16[1024,2432]{1,0:T(8,128)(2,1)} %bitcast.22), kind=kOutput, calls=%fused_computation | convolution fusion | flops 1912602624 | bytes 8421376 | tf_op jit(solution)/shard_map/dot_general | solution.py:511
  38.0 0.5 copy.12
  38.4 0.0 slice-start
  38.4 0.2 broadcast_divide_fusion.start
  38.7 0.0 slice-start.1
  38.7 1.5 %broadcast_in_dim.26.coef = f32[4,32,80,128]{3,2,1,0:T(8,128)S(1)} broadcast(f32[4,32,80]{2,1,0:T(8,128)S(1)} %pad_maximum_fusion), dimensions={0,1,2} | broadcast | bytes 5283840 | tf_op jit(solution)/shard_map/broadcast_in_dim | solution.py:510
  40.2 26.7 %shard_map.78 = (f32[16,64,384]{2,1,0:T(8,128)S(1)}, bf16[16,64,384]{2,1,0:T(8,128)(2,1)S(1)}) custom-call(f32[16,64,384]{2,1,0:T(8,128)S(1)} %broadcast_divide_fusion.start, f32[4,32,80,128]{3,2,1,0:T(8,128)S(1)} %broadcast_in_dim.26.coef), custom_call_target="tpu_custom_call" | custom-call | tf_op jit(solution)/shard_map/pallas_call | solution.py:448
  66.9 0.0 slice-done
  66.9 0.0 slice-done.1
  66.9 0.0 copy-start
  66.9 0.0 copy-start.3
  66.9 43.8 %shard_map.79 = f32[80,384]{1,0:T(8,128)S(1)} custom-call(bf16[1024,2432]{1,0:T(8,128)(2,1)S(1)} %bitcast.25, bf16[1024,384]{1,0:T(8,128)(2,1)S(1)} %bitcast.26), custom_call_target="tpu_custom_call" | custom-call | tf_op jit(solution)/shard_map/pallas_call | solution.py:320
  110.7 0.0 copy-done
  110.7 0.0 copy-done.3
  110.7 0.7 multiply_add_fusion
  111.5 1.1 %copy.17 = f32[16,64,384]{2,1,0:T(8,128)} copy(f32[16,64,384]{2,1,0:T(8,128)S(1)} %get-tuple-element.17) | data formatting | bytes 3145728
  (6 shorter events, 0.1 us)
Async XLA Ops:
  0.6 30.2 %copy-start.2 = (f32[16]{0:T(128)S(1)}, f32[16]{0:T(128)}, u32[]{:S(2)}) copy-start(f32[16]{0:T(128)} %param.11) | copy-start | bytes 196
  0.6 30.2 %copy-start.1 = (f32[16]{0:T(128)S(1)}, f32[16]{0:T(128)}, u32[]{:S(2)}) copy-start(f32[16]{0:T(128)} %param.10) | copy-start | bytes 196
  38.4 28.4 %slice-start = ((s8[4980736]{0:T(1024)(128)(4,1)}), s8[4194304]{0:T(1024)(128)(4,1)S(1)}, s32[]{:S(2)}) async-start(s8[4980736]{0:T(1024)(128)(4,1)} %bitcast.23), calls=%async_computation | async-start | bytes 8388608
  38.7 28.2 %slice-start.1 = ((s8[4980736]{0:T(1024)(128)(4,1)}), s8[786432]{0:T(1024)(128)(4,1)S(1)}, s32[]{:S(2)}) async-start(s8[4980736]{0:T(1024)(128)(4,1)} %bitcast.23), calls=%async_computation.1 | async-start | bytes 1572864
  66.9 43.8 %copy-start = (bf16[76,384]{1,0:T(8,128)(2,1)S(1)}, bf16[76,384]{1,0:T(8,128)(2,1)}, u32[]{:S(2)}) copy-start(bf16[76,384]{1,0:T(8,128)(2,1)} %param.7) | copy-start | bytes 175108
  66.9 43.8 %copy-start.3 = (f32[76]{0:T(128)S(1)}, f32[76]{0:T(128)}, u32[]{:S(2)}) copy-start(f32[76]{0:T(128)} %param.8) | copy-start | bytes 916

commit v4 on v3

--- a/solution.py
+++ b/solution.py
@@ -52,6 +52,7 @@
 
 def gather_kernel(dims, mine, full, own_sem, sz, rz, s1, r1, s2, r2, ss, rs):
     here = Place(dims)
+    Y, X, Z = dims
     me = here.core
     sib = here.device(core=1 - me)
     home = full.at[here.y, here.x, here.z, me]
@@ -59,80 +60,75 @@
     copy.start()
     here.barrier()
     copies = []
-    for d in range(1, here.Z):
+    for d in range(1, Z):
         sent = remote(mine, home, sz.at[d - 1], rz.at[d - 1], here.device(z=here.ahead("z", d)))
         sent.start()
         copies.append(sent)
     copy.wait()
-    for d in range(1, here.Z):
-        back = full.at[here.y, here.x, here.ahead("z", -d), me]
-        remote(back, back, sz.at[d - 1], rz.at[d - 1], sib).wait_recv()
     for c in (0, 1):
 
         @pl.when(me == c)
         def _():
             near, far = "xy"[c], "yx"[c]
+            n1, n2 = here.n[near], here.n[far]
             sent_here = []
 
-            def line(index, core):
-                where = {**here.at, near: index}
-                return full.at[where["y"], where["x"], :, core]
-
-            def sheet(index, core):
-                return full.at[index, :, :, core] if far == "y" else full.at[:, index, :, core]
-
-            own = line(here.at[near], c)
-            for d in range(1, here.n[near]):
-                sent = remote(
-                    own, own, s1.at[d - 1], r1.at[d - 1], here.device(**{near: here.ahead(near, d)})
-                )
+            def block(d, e, f, core):
+                x, y = ((e, f), (f, e))[c]
+                return full.at[here.ahead("y", -y), here.ahead("x", -x), here.ahead("z", -d), core]
+
+            def share_number(d, e, f):
+                x, y = ((e, f), (f, e))[c]
+                return (d * X + x) * Y + y
+
+            def start(*what):
+                sent = remote(*what)
                 sent.start()
                 sent_here.append(sent)
-            count = 0
-            share = remote(own, own, ss.at[count], rs.at[count], sib)
-            share.start()
-            sent_here.append(share)
-            for d in range(1, here.n[near]):
-                back = line(here.ahead(near, -d), c)
-                remote(back, back, s1.at[d - 1], r1.at[d - 1], sib).wait_recv()
-            own = sheet(here.at[far], c)
-            for d in range(1, here.n[far]):
-                sent = remote(
-                    own, own, s2.at[d - 1], r2.at[d - 1], here.device(**{far: here.ahead(far, d)})
-                )
-                sent.start()
-                sent_here.append(sent)
-            for d in range(1, here.n[near]):
-                count += 1
-                back = line(here.ahead(near, -d), c)
-                share = remote(back, back, ss.at[count], rs.at[count], sib)
-                share.start()
-                sent_here.append(share)
-            for d in range(1, here.n[far]):
-                back = sheet(here.ahead(far, -d), c)
-                remote(back, back, s2.at[d - 1], r2.at[d - 1], sib).wait_recv()
-                count += 1
-                share = remote(back, back, ss.at[count], rs.at[count], sib)
-                share.start()
-                sent_here.append(share)
-            near2, far2 = far, near
-            got = 0
-
-            def line2(index):
-                where = {**here.at, near2: index}
-                return full.at[where["y"], where["x"], :, 1 - c]
-
-            def sheet2(index):
-                return full.at[index, :, :, 1 - c] if far2 == "y" else full.at[:, index, :, 1 - c]
-
-            for d in range(0, here.n[near2]):
-                back = line2(here.ahead(near2, -d))
-                remote(back, back, ss.at[got], rs.at[got], sib).wait_recv()
-                got += 1
-            for d in range(1, here.n[far2]):
-                back = sheet2(here.ahead(far2, -d))
-                remote(back, back, ss.at[got], rs.at[got], sib).wait_recv()
-                got += 1
+
+            def arrived(ref, send, recv):
+                remote(ref, ref, send, recv, sib).wait_recv()
+
+            def to_far(held, d, e):
+                for f in range(1, n2):
+                    k = (d * n1 + e) * n2 + f
+                    start(
+                        held, held, s2.at[k], r2.at[k], here.device(**{far: here.ahead(far, f)})
+                    )
+
+            def to_sibling(held, d, e, f):
+                k = share_number(d, e, f)
+                start(held, held, ss.at[k], rs.at[k], sib)
+
+            for d in range(Z):
+                held = block(d, 0, 0, c)
+                if d:
+                    arrived(held, sz.at[d - 1], rz.at[d - 1])
+                for e in range(1, n1):
+                    k = d * n1 + e
+                    start(
+                        held, held, s1.at[k], r1.at[k], here.device(**{near: here.ahead(near, e)})
+                    )
+                to_far(held, d, 0)
+                to_sibling(held, d, 0, 0)
+            for d in range(Z):
+                for e in range(1, n1):
+                    held = block(d, e, 0, c)
+                    arrived(held, s1.at[d * n1 + e], r1.at[d * n1 + e])
+                    to_far(held, d, e)
+                    to_sibling(held, d, e, 0)
+            for e in range(n1):
+                for d in range(Z):
+                    for f in range(1, n2):
+                        held = block(d, e, f, c)
+                        k = (d * n1 + e) * n2 + f
+                        arrived(held, s2.at[k], r2.at[k])
+                        to_sibling(held, d, e, f)
+            for d in range(Z):
+                for e in range(n1):
+                    for f in range(n2):
+                        k = share_number(d, e, f)
+                        arrived(block(d, e, f, 1 - c), ss.at[k], rs.at[k])
             for sent in sent_here:
                 sent.wait_send()
 
@@ -151,8 +147,8 @@
         out_specs=pl.BlockSpec(memory_space=pltpu.VMEM),
         scratch_shapes=[dma]
         + [dma((max(Z - 1, 1),))] * 2
-        + [dma((widest,))] * 4
-        + [dma((X + Y,))] * 2,
+        + [dma((Z * widest,))] * 2
+        + [dma((X * Y * Z,))] * 4,
         compiler_params=pltpu.CompilerParams(
             collective_id=0, has_side_effects=True, vmem_limit_bytes=16 << 20
         ),
@@ -243,20 +239,22 @@
                     value = value + back[...]
                 held[...] = value
                 if d2:
-                    sent = remote(
-                        held, r2.at[d2 - 1], s2.at[d2 - 1], g2.at[d2 - 1],
-                        here.device(**{far: index}),
-                    )
-                    sent.start()
-                    sent_here.append(sent)
-            for d in range(1, n2):
-                remote(r2.at[d - 1], r2.at[d - 1], s2.at[d - 1], g2.at[d - 1], sib).wait_recv()
+                    for d in [*range(1, Z), 0]:
+                        z, k = here.ahead("z", d), (d2 - 1) * Z + d
+                        sent = remote(
+                            held.at[z], r2.at[d2 - 1, z], s2.at[k], g2.at[k],
+                            here.device(**{far: index}),
+                        )
+                        sent.start()
+                        sent_here.append(sent)
             for d in [*range(1, Z), 0]:
                 index = here.ahead("z", d)
                 held = total.at[here.y, here.x, index]
                 value = held[...]
                 for e in range(1, n2):
-                    value = value + r2.at[e - 1, index][...]
+                    back, k = r2.at[e - 1, index], (e - 1) * Z + d
+                    remote(back, back, s2.at[k], g2.at[k], sib).wait_recv()
+                    value = value + back[...]
                 held[...] = value
                 if d:
                     sent = remote(
@@ -324,7 +322,7 @@
         out_specs=vmem,
         scratch_shapes=scratch
         + [dma((X * Y,))] * 4
-        + [dma((widest,))] * 2
+        + [dma((widest * Z,))] * 2
         + [dma((max(Z - 1, 1),))] * 2,
         compiler_params=pltpu.CompilerParams(
             collective_id=1, has_side_effects=True, vmem_limit_bytes=40 << 20

time: 113 us -> 105 us (0.929)
  Pallas kernels: 98.3 us -> 89.7 us
    pallas_call x1, Pallas kernels: 27.9 us -> 21.7 us  [gather(): pl.pallas_call(functools.partial(gather_kernel, dims), out_shape=jax.Shap...]
    pallas_call x1, Pallas kernels: 43.8 us -> 41.3 us  [scatter(): pl.pallas_call(functools.partial(scatter_kernel, dims, (0, start), H, fus...]
where the time goes in v4:
time: 105 us; the launch traced here: 104 us
  Pallas kernels  89.7 us (85%)
  local copies, waits for them, and re-layouts  5.23 us (5%)
  matrix products  5.22 us (5%)
  other arithmetic  3.01 us (3%)
    pallas_call x1, Pallas kernels, scatter(): pl.pallas_call(functools.partial(scatter_kernel, dims, (0, start), H, fus...  41.3 us
    pallas_call x1, Pallas kernels, smoothed(): pl.pallas_call(functools.partial(smooth_kernel, (lax.axis_size('gx'), lax...  26.7 us
    pallas_call x1, Pallas kernels, gather(): pl.pallas_call(functools.partial(gather_kernel, dims), out_shape=jax.Shap...  21.7 us
    dot_general x1, matrix products, local(): source = jnp.dot(flattened, data, preferred_element_type=jnp.float32)  5.22 us

profile of v4, /device:TPU:0, one launch (start us, length us, event | category | flops | bytes accessed | tf_op | source)
XLA Modules:
  0.0 104.0 jit_solution(6875418513610643936)
XLA Ops:
  0.6 0.0 copy-start.2
  0.6 0.0 copy-start.1
  0.7 0.7 convert_element_type.17
  1.4 0.1 convert_element_type.18
  1.5 0.8 pad_maximum_fusion.1.mine
  2.3 21.7 %shard_map.77 = bf16[2,2,4,2,79,384]{5,4,3,2,1,0:T(8,128)(2,1)S(1)} custom-call(bf16[79,384]{1,0:T(8,128)(2,1)S(1)} %pad_maximum_fusion.1.mine), custom_call_target="tpu_custom_call" | custom-call | tf_op jit(solution)/shard_map/pallas_call | solution.py:143
  24.1 0.1 slice.40
  24.1 0.1 reshape.41
  24.2 0.1 convert_element_type.19
  24.4 0.1 reshape.42
  24.5 0.1 fusion.8
  24.7 0.0 copy-done.2
  24.7 0.0 copy-done.1
  24.7 0.2 select_reduce_fusion
  24.9 0.1 select_bitcast_fusion.3
  25.0 0.1 slice.60
  25.1 0.1 select_bitcast_fusion.2
  25.2 1.4 %reshape.39 = bf16[2432,384]{1,0:T(8,128)(2,1)} reshape(bf16[2,2,4,2,76,384]{5,4,3,2,1,0:T(8,128)(2,1)S(1)} %bitcast.21) | data formatting | bytes 3735552 | tf_op jit(solution)/shard_map/reshape | solution.py:492
  26.6 5.2 %convolution_bitcast_fusion = f32[1024,384]{0,1:T(8,128)S(1)} fusion(bf16[2432,384]{1,0:T(8,128)(2,1)} %reshape.39, bf16[1024,2432]{1,0:T(8,128)(2,1)} %bitcast.22), kind=kOutput, calls=%fused_computation | convolution fusion | flops 1912602624 | bytes 8421376 | tf_op jit(solution)/shard_map/dot_general | solution.py:509
  31.8 0.5 copy.12
  32.3 0.0 slice-start
  32.3 0.2 broadcast_divide_fusion.start
  32.5 0.0 slice-start.1
  32.5 1.5 %broadcast_in_dim.26.coef = f32[4,32,80,128]{3,2,1,0:T(8,128)S(1)} broadcast(f32[4,32,80]{2,1,0:T(8,128)S(1)} %pad_maximum_fusion), dimensions={0,1,2} | broadcast | bytes 5283840 | tf_op jit(solution)/shard_map/broadcast_in_dim | solution.py:508
  34.1 26.7 %shard_map.78 = (f32[16,64,384]{2,1,0:T(8,128)S(1)}, bf16[16,64,384]{2,1,0:T(8,128)(2,1)S(1)}) custom-call(f32[16,64,384]{2,1,0:T(8,128)S(1)} %broadcast_divide_fusion.start, f32[4,32,80,128]{3,2,1,0:T(8,128)S(1)} %broadcast_in_dim.26.coef), custom_call_target="tpu_custom_call" | custom-call | tf_op jit(solution)/shard_map/pallas_call | solution.py:446
  60.7 0.0 slice-done
  60.7 0.0 slice-done.1
  60.8 0.0 copy-start
  60.8 0.0 copy-start.3
  60.8 41.3 %shard_map.79 = f32[80,384]{1,0:T(8,128)S(1)} custom-call(bf16[1024,2432]{1,0:T(8,128)(2,1)S(1)} %bitcast.25, bf16[1024,384]{1,0:T(8,128)(2,1)S(1)} %bitcast.26), custom_call_target="tpu_custom_call" | custom-call | tf_op jit(solution)/shard_map/pallas_call | solution.py:318
  102.1 0.0 copy-done
  102.1 0.0 copy-done.3
  102.1 0.7 multiply_add_fusion
  102.8 1.1 %copy.17 = f32[16,64,384]{2,1,0:T(8,128)} copy(f32[16,64,384]{2,1,0:T(8,128)S(1)} %get-tuple-element.17) | data formatting | bytes 3145728
  (6 shorter events, 0.1 us)
Async XLA Ops:
  0.6 24.0 %copy-start.2 = (f32[16]{0:T(128)S(1)}, f32[16]{0:T(128)}, u32[]{:S(2)}) copy-start(f32[16]{0:T(128)} %param.11) | copy-start | bytes 196
  0.6 24.0 %copy-start.1 = (f32[16]{0:T(128)S(1)}, f32[16]{0:T(128)}, u32[]{:S(2)}) copy-start(f32[16]{0:T(128)} %param.10) | copy-start | bytes 196
  32.3 28.4 %slice-start = ((s8[4980736]{0:T(1024)(128)(4,1)}), s8[4194304]{0:T(1024)(128)(4,1)S(1)}, s32[]{:S(2)}) async-start(s8[4980736]{0:T(1024)(128)(4,1)} %bitcast.23), calls=%async_computation | async-start | bytes 8388608
  32.5 28.2 %slice-start.1 = ((s8[4980736]{0:T(1024)(128)(4,1)}), s8[786432]{0:T(1024)(128)(4,1)S(1)}, s32[]{:S(2)}) async-start(s8[4980736]{0:T(1024)(128)(4,1)} %bitcast.23), calls=%async_computation.1 | async-start | bytes 1572864
  60.8 41.3 %copy-start = (bf16[76,384]{1,0:T(8,128)(2,1)S(1)}, bf16[76,384]{1,0:T(8,128)(2,1)}, u32[]{:S(2)}) copy-start(bf16[76,384]{1,0:T(8,128)(2,1)} %param.7) | copy-start | bytes 175108
  60.8 41.3 %copy-start.3 = (f32[76]{0:T(128)S(1)}, f32[76]{0:T(128)}, u32[]{:S(2)}) copy-start(f32[76]{0:T(128)} %param.8) | copy-start | bytes 916

commit v5 on v4

--- a/solution.py
+++ b/solution.py
@@ -219,28 +219,31 @@
                 held[...] = part[y, x, :, pl.ds(starts[c], H), :] + arrived[...]
                 d = (dx, dy)[c]
                 if d:
-                    sent = remote(
-                        held,
-                        r1.at[d - 1, (y, x)[c]],
-                        s1.at[number],
-                        g1.at[number],
-                        here.device(**{near: (x, y)[c]}),
-                    )
-                    sent.start()
-                    sent_here.append(sent)
+                    for dz in [*range(1, Z), 0]:
+                        z, k = here.ahead("z", dz), number * Z + dz
+                        sent = remote(
+                            held.at[z],
+                            r1.at[d - 1, (y, x)[c], z],
+                            s1.at[k],
+                            g1.at[k],
+                            here.device(**{near: (x, y)[c]}),
+                        )
+                        sent.start()
+                        sent_here.append(sent)
             for d2 in [*range(1, n2), 0]:
                 index = here.ahead(far, d2)
                 held = total.at[(index, here.x) if c == 0 else (here.y, index)]
-                value = held[...]
-                for d in range(1, n1):
-                    number = order.index((d2, d) if c == 0 else (d, d2))
-                    back = r1.at[d - 1, index]
-                    remote(back, back, s1.at[number], g1.at[number], sib).wait_recv()
-                    value = value + back[...]
-                held[...] = value
-                if d2:
-                    for d in [*range(1, Z), 0]:
-                        z, k = here.ahead("z", d), (d2 - 1) * Z + d
+                for dz in [*range(1, Z), 0]:
+                    z = here.ahead("z", dz)
+                    value = held[z]
+                    for d in range(1, n1):
+                        k = order.index((d2, d) if c == 0 else (d, d2)) * Z + dz
+                        back = r1.at[d - 1, index, z]
+                        remote(back, back, s1.at[k], g1.at[k], sib).wait_recv()
+                        value = value + back[...]
+                    held[z] = value
+                    if d2:
+                        k = (d2 - 1) * Z + dz
                         sent = remote(
                             held.at[z], r2.at[d2 - 1, z], s2.at[k], g2.at[k],
                             here.device(**{far: index}),
@@ -321,7 +324,7 @@
         in_specs=[vmem] * len(given),
         out_specs=vmem,
         scratch_shapes=scratch
-        + [dma((X * Y,))] * 4
+        + [dma((X * Y * Z,))] * 4
         + [dma((widest * Z,))] * 2
         + [dma((max(Z - 1, 1),))] * 2,
         compiler_params=pltpu.CompilerParams(

time: 105 us -> 107 us (1.019)
  Pallas kernels: 89.7 us -> 91 us
    pallas_call x1, Pallas kernels: 41.3 us -> 42.6 us  [scatter(): pl.pallas_call(functools.partial(scatter_kernel, dims, (0, start), H, fus...]
where the time goes in v5:
time: 107 us; the launch traced here: 105 us
  Pallas kernels  91 us (85%)
  local copies, waits for them, and re-layouts  5.23 us (5%)
  matrix products  5.22 us (5%)
  other arithmetic  3.01 us (3%)
    pallas_call x1, Pallas kernels, scatter(): pl.pallas_call(functools.partial(scatter_kernel, dims, (0, start), H, fus...  42.6 us
    pallas_call x1, Pallas kernels, smoothed(): pl.pallas_call(functools.partial(smooth_kernel, (lax.axis_size('gx'), lax...  26.7 us
    pallas_call x1, Pallas kernels, gather(): pl.pallas_call(functools.partial(gather_kernel, dims), out_shape=jax.Shap...  21.7 us
    dot_general x1, matrix products, local(): source = jnp.dot(flattened, data, preferred_element_type=jnp.float32)  5.22 us

profile of v5, /device:TPU:0, one launch (start us, length us, event | category | flops | bytes accessed | tf_op | source)
XLA Modules:
  0.0 105.3 jit_solution(4778866719706848293)
XLA Ops:
  0.6 0.0 copy-start.2
  0.6 0.0 copy-start.1
  0.7 0.7 convert_element_type.17
  1.4 0.1 convert_element_type.18
  1.5 0.8 pad_maximum_fusion.1.mine
  2.3 21.7 %shard_map.77 = bf16[2,2,4,2,79,384]{5,4,3,2,1,0:T(8,128)(2,1)S(1)} custom-call(bf16[79,384]{1,0:T(8,128)(2,1)S(1)} %pad_maximum_fusion.1.mine), custom_call_target="tpu_custom_call" | custom-call | tf_op jit(solution)/shard_map/pallas_call | solution.py:143
  24.1 0.1 slice.40
  24.1 0.1 reshape.41
  24.2 0.1 convert_element_type.19
  24.4 0.1 reshape.42
  24.5 0.1 fusion.8
  24.7 0.0 copy-done.2
  24.7 0.0 copy-done.1
  24.7 0.2 select_reduce_fusion
  24.9 0.1 select_bitcast_fusion.3
  25.0 0.1 slice.60
  25.1 0.1 select_bitcast_fusion.2
  25.2 1.4 %reshape.39 = bf16[2432,384]{1,0:T(8,128)(2,1)} reshape(bf16[2,2,4,2,76,384]{5,4,3,2,1,0:T(8,128)(2,1)S(1)} %bitcast.21) | data formatting | bytes 3735552 | tf_op jit(solution)/shard_map/reshape | solution.py:495
  26.6 5.2 %convolution_bitcast_fusion = f32[1024,384]{0,1:T(8,128)S(1)} fusion(bf16[2432,384]{1,0:T(8,128)(2,1)} %reshape.39, bf16[1024,2432]{1,0:T(8,128)(2,1)} %bitcast.22), kind=kOutput, calls=%fused_computation | convolution fusion | flops 1912602624 | bytes 8421376 | tf_op jit(solution)/shard_map/dot_general | solution.py:512
  31.8 0.5 copy.12
  32.3 0.0 slice-start
  32.3 0.2 broadcast_divide_fusion.start
  32.5 0.0 slice-start.1
  32.5 1.5 %broadcast_in_dim.26.coef = f32[4,32,80,128]{3,2,1,0:T(8,128)S(1)} broadcast(f32[4,32,80]{2,1,0:T(8,128)S(1)} %pad_maximum_fusion), dimensions={0,1,2} | broadcast | bytes 5283840 | tf_op jit(solution)/shard_map/broadcast_in_dim | solution.py:511
  34.1 26.7 %shard_map.78 = (f32[16,64,384]{2,1,0:T(8,128)S(1)}, bf16[16,64,384]{2,1,0:T(8,128)(2,1)S(1)}) custom-call(f32[16,64,384]{2,1,0:T(8,128)S(1)} %broadcast_divide_fusion.start, f32[4,32,80,128]{3,2,1,0:T(8,128)S(1)} %broadcast_in_dim.26.coef), custom_call_target="tpu_custom_call" | custom-call | tf_op jit(solution)/shard_map/pallas_call | solution.py:449
  60.7 0.0 slice-done
  60.7 0.0 slice-done.1
  60.8 0.0 copy-start
  60.8 0.0 copy-start.3
  60.8 42.6 %shard_map.79 = f32[80,384]{1,0:T(8,128)S(1)} custom-call(bf16[1024,2432]{1,0:T(8,128)(2,1)S(1)} %bitcast.25, bf16[1024,384]{1,0:T(8,128)(2,1)S(1)} %bitcast.26), custom_call_target="tpu_custom_call" | custom-call | tf_op jit(solution)/shard_map/pallas_call | solution.py:321
  103.4 0.0 copy-done
  103.4 0.0 copy-done.3
  103.4 0.7 multiply_add_fusion
  104.1 1.1 %copy.17 = f32[16,64,384]{2,1,0:T(8,128)} copy(f32[16,64,384]{2,1,0:T(8,128)S(1)} %get-tuple-element.17) | data formatting | bytes 3145728
  (6 shorter events, 0.1 us)
Async XLA Ops:
  0.6 24.0 %copy-start.2 = (f32[16]{0:T(128)S(1)}, f32[16]{0:T(128)}, u32[]{:S(2)}) copy-start(f32[16]{0:T(128)} %param.11) | copy-start | bytes 196
  0.6 24.0 %copy-start.1 = (f32[16]{0:T(128)S(1)}, f32[16]{0:T(128)}, u32[]{:S(2)}) copy-start(f32[16]{0:T(128)} %param.10) | copy-start | bytes 196
  32.3 28.4 %slice-start = ((s8[4980736]{0:T(1024)(128)(4,1)}), s8[4194304]{0:T(1024)(128)(4,1)S(1)}, s32[]{:S(2)}) async-start(s8[4980736]{0:T(1024)(128)(4,1)} %bitcast.23), calls=%async_computation | async-start | bytes 8388608
  32.5 28.2 %slice-start.1 = ((s8[4980736]{0:T(1024)(128)(4,1)}), s8[786432]{0:T(1024)(128)(4,1)S(1)}, s32[]{:S(2)}) async-start(s8[4980736]{0:T(1024)(128)(4,1)} %bitcast.23), calls=%async_computation.1 | async-start | bytes 1572864
  60.8 42.6 %copy-start = (bf16[76,384]{1,0:T(8,128)(2,1)S(1)}, bf16[76,384]{1,0:T(8,128)(2,1)}, u32[]{:S(2)}) copy-start(bf16[76,384]{1,0:T(8,128)(2,1)} %param.7) | copy-start | bytes 175108
  60.8 42.6 %copy-start.3 = (f32[76]{0:T(128)S(1)}, f32[76]{0:T(128)}, u32[]{:S(2)}) copy-start(f32[76]{0:T(128)} %param.8) | copy-start | bytes 916
